TPU v7x, 32 devices: a whole 2x2x4 slice. The times are simulated.
32 devices in a mesh: dp: 2 (over core), seq: 16 (over z, y, x).
Axes of the slice: x: 2, y: 2, z: 4, core: 2. Of those that a mesh axis runs over, the one named last changes fastest.
Arguments:
- hidden_in: bfloat16 [4, 4096, 768], P('dp', 'seq'), may hold values from -6 to 6
- cotangent: bfloat16 [4, 4096, 768], P('dp', 'seq'), may hold values from -6 to 6
- segments: int32 [4, 4096], P('dp'), may hold values from 0 to 20, as said below
- pad_mask: int32 [4, 4096], P('dp'), may hold values 0 or 1
- w_qkv: bfloat16 [768, 2304], P(('dp', 'seq')), may hold values from -0.21875 to 0.21875
- b_query: bfloat16 [768], P(('dp', 'seq')), may hold values from -3 to 3
- b_value: bfloat16 [768], P(('dp', 'seq')), may hold values from -3 to 3
- w_out: bfloat16 [768, 768], P(('dp', 'seq')), may hold values from -0.875 to 0.875
- b_out: bfloat16 [768], P(('dp', 'seq')), may hold values from -3 to 3
- norm1_gain: bfloat16 [768], P(('dp', 'seq')), may hold values from 0.099609375 to 1.8984375
- norm1_bias: bfloat16 [768], P(('dp', 'seq')), may hold values from -3 to 3
- w_up: bfloat16 [768, 3072], P(('dp', 'seq')), may hold values from -0.21875 to 0.21875
- b_up: bfloat16 [3072], P(('dp', 'seq')), may hold values from -3 to 3
- w_down: bfloat16 [3072, 768], P(('dp', 'seq')), may hold values from -0.109375 to 0.109375
- b_down: bfloat16 [768], P(('dp', 'seq')), may hold values from -3 to 3
- norm2_gain: bfloat16 [768], P(('dp', 'seq')), may hold values from 0.099609375 to 1.8984375
- norm2_bias: bfloat16 [768], P(('dp', 'seq')), may hold values from -3 to 3
Outputs:
- hidden_out: bfloat16 [4, 4096, 768], P('dp', 'seq')
- hidden_grad: float32 [4, 4096, 768], P('dp', 'seq')
- grad_w_qkv: float32 [768, 2304], P(('dp', 'seq'))
- grad_b_query: float32 [768], P(('dp', 'seq'))
- grad_b_value: float32 [768], P(('dp', 'seq'))
- grad_w_out: float32 [768, 768], P(('dp', 'seq'))
- grad_b_out: float32 [768], P(('dp', 'seq'))
- grad_norm1_gain: float32 [768], P(('dp', 'seq'))
- grad_norm1_bias: float32 [768], P(('dp', 'seq'))
- grad_w_up: float32 [768, 3072], P(('dp', 'seq'))
- grad_b_up: float32 [3072], P(('dp', 'seq'))
- grad_w_down: float32 [3072, 768], P(('dp', 'seq'))
- grad_b_down: float32 [768], P(('dp', 'seq'))
- grad_norm2_gain: float32 [768], P(('dp', 'seq'))
- grad_norm2_bias: float32 [768], P(('dp', 'seq'))
Inputs may be any that keep to these rules, and one draw needn't show every extreme that they name: `segments`: along a sequence the numbers never fall and change exactly where a document ends; the documents before the last carry 0, 1, 2 and so on, and the last document of every sequence carries 21 - 1; every document has 200 to 768 tokens except the last of a sequence, which may be cut short; one of the first two documents of every sequence has exactly 768 tokens.
All inputs are finite; a program needn't handle non-finite values. No bound on the sum of `pad_mask` on one device may be relied on, other than what follows from the above.
Results may differ from a plain program's by a relative error of at most 0.015.
Values may be sent and summed in bfloat16 or wider, within the bound.
A program may use at most 320 MiB of HBM per device.

v0:
```python
import jax
import jax.numpy as jnp
from jax import lax
from jax.sharding import PartitionSpec as P

HEADS = 12
HEAD = 64
REACH = 3


def from_behind(block, axis, distance):
    devices = range(lax.axis_size(axis))
    route = [(i - distance, i) for i in devices if i - distance in devices]
    return lax.ppermute(block, axis, route)


def normalize(resid, gain, shift):
    center = resid - jnp.mean(resid, axis=-1, keepdims=True)
    spread = jnp.mean(center * center, axis=-1, keepdims=True)
    return center * lax.rsqrt(spread + 1e-12) * gain + shift


def exact_gelu(values):
    return jax.nn.gelu(values, approximate=False)


def outer_product(left, right):
    return lax.dot_general(
        left, right, (((0,), (0,)), ((), ())), preferred_element_type=jnp.float32
    )


def back_product(left, matrix):
    return lax.dot_general(
        left, matrix, (((1,), (1,)), ((), ())), preferred_element_type=jnp.float32
    )


def build_mask(seg_row, pad_row, shard_rows, device_rank):
    margin = REACH * shard_rows
    window = (2 * REACH + 1) * shard_rows
    offset = device_rank * shard_rows
    seg_keys = lax.dynamic_slice_in_dim(
        jnp.pad(seg_row, (margin, margin), constant_values=-1), offset, window
    )
    mask_keys = lax.dynamic_slice_in_dim(jnp.pad(pad_row, (margin, margin)), offset, window)
    seg_query = lax.dynamic_slice_in_dim(seg_row, offset, shard_rows)
    pad_query = lax.dynamic_slice_in_dim(pad_row, offset, shard_rows)
    itself = jnp.arange(shard_rows)[:, None] + margin == jnp.arange(window)[None, :]
    allowed = (seg_query[:, None] == seg_keys[None, :]) & ((mask_keys[None, :] == 1) | itself)
    return (allowed, pad_query)


def collect_window(pairs):
    earlier = [from_behind(pairs, "seq", distance) for distance in range(REACH, 0, -1)]
    later = [from_behind(pairs, "seq", -distance) for distance in range(1, REACH + 1)]
    return jnp.concatenate(earlier + [pairs] + later, axis=0)


def group_slices(projected, window_kv, group):
    model_dim = projected.shape[1] // 3
    width = 2 * HEAD
    column = group * width
    queries = lax.dynamic_slice_in_dim(projected, column, width, 1).reshape(
        projected.shape[0], 2, HEAD
    )
    keys_grp = lax.dynamic_slice_in_dim(window_kv, column, width, 1).reshape(
        window_kv.shape[0], 2, HEAD
    )
    values_grp = lax.dynamic_slice_in_dim(window_kv, model_dim + column, width, 1).reshape(
        window_kv.shape[0], 2, HEAD
    )
    return (queries, keys_grp, values_grp)


def score_block(queries, keys_grp, allowed):
    scores = (
        jnp.einsum("qhd,khd->hqk", queries, keys_grp, preferred_element_type=jnp.float32) * 0.125
    )
    return jnp.where(allowed[None], scores, -1e30)


def forward_layer(state, full, allowed):
    (
        mat_qkv,
        bias_query,
        bias_value,
        mat_out,
        bias_out,
        gain_one,
        shift_one,
        mat_up,
        bias_up,
        mat_down,
        bias_down,
        gain_two,
        shift_two,
    ) = full
    shard_rows, model_dim = state.shape
    state_low = state.astype(jnp.bfloat16)
    bias_all = jnp.concatenate(
        [
            bias_query.astype(jnp.float32),
            jnp.zeros((model_dim,), jnp.float32),
            bias_value.astype(jnp.float32),
        ]
    )
    projected = (jnp.dot(state_low, mat_qkv, preferred_element_type=jnp.float32) + bias_all).astype(
        jnp.bfloat16
    )
    window_kv = collect_window(projected[:, model_dim:])

    def attend(group):
        queries, keys_grp, values_grp = group_slices(projected, window_kv, group)
        scores = score_block(queries, keys_grp, allowed)
        top = jnp.max(scores, axis=-1, keepdims=True)
        expo = jnp.exp(scores - top)
        total = jnp.sum(expo, axis=-1, keepdims=True)
        probs = (expo / total).astype(jnp.bfloat16)
        context_grp = jnp.einsum(
            "hqk,khd->qhd", probs, values_grp, preferred_element_type=jnp.float32
        )
        return (
            context_grp.reshape(shard_rows, 2 * HEAD).astype(jnp.bfloat16),
            top + jnp.log(total),
        )

    contexts, log_total = lax.map(attend, jnp.arange(HEADS // 2, dtype=jnp.int32))
    context = jnp.transpose(contexts, (1, 0, 2)).reshape(shard_rows, model_dim)
    attn = jnp.dot(context, mat_out, preferred_element_type=jnp.float32) + bias_out.astype(
        jnp.float32
    )
    resid_one = state + attn
    hidden = normalize(resid_one, gain_one.astype(jnp.float32), shift_one.astype(jnp.float32))
    hidden_low = hidden.astype(jnp.bfloat16)
    up_pre = jnp.dot(hidden_low, mat_up, preferred_element_type=jnp.float32) + bias_up.astype(
        jnp.float32
    )
    active = exact_gelu(up_pre).astype(jnp.bfloat16)
    ffn = jnp.dot(active, mat_down, preferred_element_type=jnp.float32) + bias_down.astype(
        jnp.float32
    )
    resid_two = hidden + ffn
    result = normalize(resid_two, gain_two.astype(jnp.float32), shift_two.astype(jnp.float32))
    saved = (
        state_low,
        projected,
        window_kv,
        log_total,
        context,
        resid_one,
        hidden_low,
        up_pre,
        active,
        resid_two,
    )
    return (result, saved)


def backward_layer(grad_out, full, saved, allowed):
    (
        mat_qkv,
        bias_query,
        bias_value,
        mat_out,
        bias_out,
        gain_one,
        shift_one,
        mat_up,
        bias_up,
        mat_down,
        bias_down,
        gain_two,
        shift_two,
    ) = full
    (
        state_low,
        projected,
        kept_window,
        log_total,
        context,
        resid_one,
        hidden_low,
        up_pre,
        active,
        resid_two,
    ) = saved
    shard_rows, model_dim = resid_one.shape
    _, back_two = jax.vjp(
        normalize, resid_two, gain_two.astype(jnp.float32), shift_two.astype(jnp.float32)
    )
    grad_resid2, grad_gain2, grad_shift2 = back_two(grad_out)
    grad_ffn = grad_resid2.astype(jnp.bfloat16)
    grad_bdown = jnp.sum(grad_ffn.astype(jnp.float32), axis=0)
    grad_wdown = outer_product(active, grad_ffn)
    grad_active = back_product(grad_ffn, mat_down)
    _, gelu_back = jax.vjp(exact_gelu, up_pre)
    grad_up = gelu_back(grad_active)[0].astype(jnp.bfloat16)
    grad_wup = outer_product(hidden_low, grad_up)
    grad_bup = jnp.sum(grad_up.astype(jnp.float32), axis=0)
    grad_hidden = grad_resid2 + back_product(grad_up, mat_up)
    _, back_one = jax.vjp(
        normalize, resid_one, gain_one.astype(jnp.float32), shift_one.astype(jnp.float32)
    )
    grad_resid1, grad_gain1, grad_shift1 = back_one(grad_hidden)
    grad_attn = grad_resid1.astype(jnp.bfloat16)
    grad_wout = outer_product(context, grad_attn)
    grad_bout = jnp.sum(grad_attn.astype(jnp.float32), axis=0)
    grad_context = back_product(grad_attn, mat_out).astype(jnp.bfloat16)
    window = kept_window.shape[0]

    def attend_back(group):
        queries, keys_grp, values_grp = group_slices(projected, kept_window, group)
        scores = score_block(queries, keys_grp, allowed)
        probs = jnp.exp(scores - log_total[group])
        grad_ctx = lax.dynamic_slice_in_dim(grad_context, group * 2 * HEAD, 2 * HEAD, 1).reshape(
            shard_rows, 2, HEAD
        )
        grad_probs = jnp.einsum(
            "qhd,khd->hqk", grad_ctx, values_grp, preferred_element_type=jnp.float32
        )
        grad_values = jnp.einsum(
            "hqk,qhd->khd", probs.astype(jnp.bfloat16), grad_ctx, preferred_element_type=jnp.float32
        )
        inner = jnp.sum(grad_probs * probs, axis=-1, keepdims=True)
        grad_scores = (probs * (grad_probs - inner)).astype(jnp.bfloat16)
        grad_queries = (
            jnp.einsum("hqk,khd->qhd", grad_scores, keys_grp, preferred_element_type=jnp.float32)
            * 0.125
        )
        grad_keys = (
            jnp.einsum("hqk,qhd->khd", grad_scores, queries, preferred_element_type=jnp.float32)
            * 0.125
        )
        return (
            grad_queries.reshape(shard_rows, 2 * HEAD),
            grad_keys.reshape(window, 2 * HEAD),
            grad_values.reshape(window, 2 * HEAD),
        )

    grad_q_groups, grad_k_groups, grad_v_groups = lax.map(
        attend_back, jnp.arange(HEADS // 2, dtype=jnp.int32)
    )
    grad_queries = jnp.transpose(grad_q_groups, (1, 0, 2)).reshape(shard_rows, model_dim)
    grad_keys = jnp.transpose(grad_k_groups, (1, 0, 2)).reshape(window, model_dim)
    grad_values = jnp.transpose(grad_v_groups, (1, 0, 2)).reshape(window, model_dim)
    grad_window = jnp.concatenate([grad_keys, grad_values], axis=1)
    grad_pairs = grad_window[REACH * shard_rows : (REACH + 1) * shard_rows]
    for distance in range(1, REACH + 1):
        earlier_piece = grad_window[
            (REACH - distance) * shard_rows : (REACH - distance + 1) * shard_rows
        ]
        later_piece = grad_window[
            (REACH + distance) * shard_rows : (REACH + distance + 1) * shard_rows
        ]
        grad_pairs = grad_pairs + from_behind(
            earlier_piece.astype(jnp.bfloat16), "seq", -distance
        ).astype(earlier_piece.dtype)
        grad_pairs = grad_pairs + from_behind(
            later_piece.astype(jnp.bfloat16), "seq", distance
        ).astype(later_piece.dtype)
    grad_proj = jnp.concatenate([grad_queries, grad_pairs], axis=1).astype(jnp.bfloat16)
    grad_wqkv = outer_product(state_low, grad_proj)
    column_sums = jnp.sum(grad_proj.astype(jnp.float32), axis=0)
    grad_state = grad_resid1 + back_product(grad_proj, mat_qkv)
    grads = (
        grad_wqkv,
        column_sums[:model_dim],
        column_sums[2 * model_dim :],
        grad_wout,
        grad_bout,
        grad_gain1,
        grad_shift1,
        grad_wup,
        grad_bup,
        grad_wdown,
        grad_bdown,
        grad_gain2,
        grad_shift2,
    )
    return (grad_state, grads)


def per_device(
    hidden_in,
    cotangent,
    segments,
    pad_mask,
    w_qkv,
    b_query,
    b_value,
    w_out,
    b_out,
    norm1_gain,
    norm1_bias,
    w_up,
    b_up,
    w_down,
    b_down,
    norm2_gain,
    norm2_bias,
):
    shards = (
        w_qkv,
        b_query,
        b_value,
        w_out,
        b_out,
        norm1_gain,
        norm1_bias,
        w_up,
        b_up,
        w_down,
        b_down,
        norm2_gain,
        norm2_bias,
    )
    group = lax.axis_size(("dp", "seq"))
    device_rank = lax.axis_index("seq")
    batches, shard_rows, model_dim = hidden_in.shape
    totals = tuple(
        (jnp.zeros((shard.shape[0] * group,) + shard.shape[1:], jnp.float32) for shard in shards)
    )
    outputs = []
    input_grads = []
    for batch in range(batches):
        allowed, pad_query = build_mask(segments[batch], pad_mask[batch], shard_rows, device_rank)
        full = (
            lax.all_gather(w_qkv, ("dp", "seq"), axis=0, tiled=True),
            lax.all_gather(b_query, ("dp", "seq"), axis=0, tiled=True),
            lax.all_gather(b_value, ("dp", "seq"), axis=0, tiled=True),
            lax.all_gather(w_out, ("dp", "seq"), axis=0, tiled=True),
            lax.all_gather(b_out, ("dp", "seq"), axis=0, tiled=True),
            lax.all_gather(norm1_gain, ("dp", "seq"), axis=0, tiled=True),
            lax.all_gather(norm1_bias, ("dp", "seq"), axis=0, tiled=True),
            lax.all_gather(w_up, ("dp", "seq"), axis=0, tiled=True),
            lax.all_gather(b_up, ("dp", "seq"), axis=0, tiled=True),
            lax.all_gather(w_down, ("dp", "seq"), axis=0, tiled=True),
            lax.all_gather(b_down, ("dp", "seq"), axis=0, tiled=True),
            lax.all_gather(norm2_gain, ("dp", "seq"), axis=0, tiled=True),
            lax.all_gather(norm2_bias, ("dp", "seq"), axis=0, tiled=True),
        )
        state_zero = hidden_in[batch].astype(jnp.float32)
        state_one, saved_one = forward_layer(state_zero, full, allowed)
        state_two, saved_two = forward_layer(state_one, full, allowed)
        grad_out = cotangent[batch].astype(jnp.float32) * pad_query[:, None].astype(jnp.float32)
        grad_mid, grads_two = backward_layer(grad_out, full, saved_two, allowed)
        grad_first, grads_one = backward_layer(grad_mid, full, saved_one, allowed)
        totals = jax.tree.map(
            lambda left, right, extra: left + right + extra, totals, grads_two, grads_one
        )
        outputs.append(state_two.astype(jnp.bfloat16))
        input_grads.append(grad_first)
    summed = (
        lax.psum_scatter(totals[0], ("dp", "seq"), scatter_dimension=0, tiled=True),
        lax.psum_scatter(totals[1], ("dp", "seq"), scatter_dimension=0, tiled=True),
        lax.psum_scatter(totals[2], ("dp", "seq"), scatter_dimension=0, tiled=True),
        lax.psum_scatter(totals[3], ("dp", "seq"), scatter_dimension=0, tiled=True),
        lax.psum_scatter(totals[4], ("dp", "seq"), scatter_dimension=0, tiled=True),
        lax.psum_scatter(totals[5], ("dp", "seq"), scatter_dimension=0, tiled=True),
        lax.psum_scatter(totals[6], ("dp", "seq"), scatter_dimension=0, tiled=True),
        lax.psum_scatter(totals[7], ("dp", "seq"), scatter_dimension=0, tiled=True),
        lax.psum_scatter(totals[8], ("dp", "seq"), scatter_dimension=0, tiled=True),
        lax.psum_scatter(totals[9], ("dp", "seq"), scatter_dimension=0, tiled=True),
        lax.psum_scatter(totals[10], ("dp", "seq"), scatter_dimension=0, tiled=True),
        lax.psum_scatter(totals[11], ("dp", "seq"), scatter_dimension=0, tiled=True),
        lax.psum_scatter(totals[12], ("dp", "seq"), scatter_dimension=0, tiled=True),
    )
    return (
        jnp.stack(outputs),
        jnp.stack(input_grads),
        summed[0],
        summed[1],
        summed[2],
        summed[3],
        summed[4],
        summed[5],
        summed[6],
        summed[7],
        summed[8],
        summed[9],
        summed[10],
        summed[11],
        summed[12],
    )


def solution(mesh):
    placed = (
        P("dp", "seq", None),
        P("dp", "seq", None),
        P("dp", None),
        P("dp", None),
        P(("dp", "seq"), None),
        P(("dp", "seq")),
        P(("dp", "seq")),
        P(("dp", "seq"), None),
        P(("dp", "seq")),
        P(("dp", "seq")),
        P(("dp", "seq")),
        P(("dp", "seq"), None),
        P(("dp", "seq")),
        P(("dp", "seq"), None),
        P(("dp", "seq")),
        P(("dp", "seq")),
        P(("dp", "seq")),
    )
    return jax.shard_map(
        per_device,
        mesh=mesh,
        in_specs=placed,
        out_specs=(
            P("dp", "seq", None),
            P("dp", "seq", None),
            P(("dp", "seq"), None),
            P(("dp", "seq")),
            P(("dp", "seq")),
            P(("dp", "seq"), None),
            P(("dp", "seq")),
            P(("dp", "seq")),
            P(("dp", "seq")),
            P(("dp", "seq"), None),
            P(("dp", "seq")),
            P(("dp", "seq"), None),
            P(("dp", "seq")),
            P(("dp", "seq")),
            P(("dp", "seq")),
        ),
        check_vma=False,
    )
```

profile of v0, /device:TPU:0, one launch (start us, length us, event | category | flops | bytes accessed | tf_op | source)
XLA Modules:
  0.0 1865.8 jit_solution(549908714064551714)
XLA Ops:
  17.6 42.4 %all-reduce.23 = (bf16[3072]{0:T(1024)(128)(2,1)S(1)}, bf16[768]{0:T(1024)(128)(2,1)S(1)}, bf16[768]{0:T(1024)(128)(2,1)S(1)}, bf16[768]{0:T(1024)(128)(2,1)S(1)...) all-reduce(bf16[3072]{0:T(1024)(128)(2,1)S(1)} %dynamic-update-slic, ...), channel_id=1, replica_groups=mesh['dp'=2,'seq'=16] {'dp','seq'}, use_global_device_ids=true, to_apply=%add.9 | all-reduce | flops 9216 | bytes 36864
  62.5 11.3 all-gather.5.cloned.1.call-done
  99.2 34.5 %collective-permute-done.12 = bf16[256,1536]{1,0:T(8,128)(2,1)} collective-permute-done((bf16[256,1536]{1,0:T(8,128)(2,1)}, bf16[256,1536]{1,0:T(8,128)(2,1)}, u32[]{:S(2)}, u32[]{:S(2)}) %collective-permute-start.12) | collective-permute-done | bytes 786464 | tf_op jit(solution)/shard_map/ppermute | solution.py:14
  137.1 19.5 %collective-permute-start = (bf16[256,1536]{1,0:T(8,128)(2,1)}, bf16[256,1536]{1,0:T(8,128)(2,1)}, u32[]{:S(2)}, u32[]{:S(2)}) collective-permute-start(bf16[256,1536]{1,0:T(8,128)(2,1)} %slice.216), channel_id=1, source_target_pairs={{0,3},{1,4},{2,5},{3,6},{4,7},{5,8},{6,9},{7,10},{8,11},{9,12},{10... | collective-permute-start | bytes 2359304 | tf_op jit(solution)/shard_map/ppermute | solution.py:14
  158.7 9.8 collective-permute-done.14
  185.8 8.3 copy.58
  194.2 39.9 %while.130 = (s32[]{:T(128)}, bf16[6,256,128]{1,2,0:T(8,128)(2,1)S(1)}, f32[6,2,256,1]{2,1,3,0:T(2,128)S(1)}, s32[6]{0:T(128)S(1)}, bf16[1792,1536]{0,1:T(8,128)...) while((s32[]{:T(128)}, ...), condition=%wide.region_19.20_spmd.clone, body=%wide.region_16.19_spmd.clone.sunk | while | flops 244088320 | bytes 15100966 | solution.py:128
  245.8 11.9 collective-permute-done.5
  258.7 8.1 copy.54
  266.9 40.0 %while.128 = (s32[]{:T(128)}, bf16[6,256,128]{1,2,0:T(8,128)(2,1)S(1)}, f32[6,2,256,1]{2,1,3,0:T(2,128)S(1)}, s32[6]{0:T(128)S(1)}, bf16[1792,1536]{0,1:T(8,128)...) while((s32[]{:T(128)}, ...), condition=%wide.region_3.4_spmd.clone, body=%wide.region_0.3_spmd.clone.sunk | while | flops 244088320 | bytes 15100966 | solution.py:128
  311.2 11.6 multiply_convert_fusion.5
  322.8 40.1 %all-gather.11.cloned.1.call-done = bf16[3072,768]{1,0:T(8,128)(2,1)} async-done(((bf16[96,768]{1,0:T(8,128)(2,1)}), bf16[3072,768]{1,0:T(8,128)(2,1)}) %all-gather.11.cloned.1.call-update) | async-done | bytes 4718608 | tf_op jit(solution)/shard_map/all_gather | solution.py:338
  386.4 11.0 multiply_convert_fusion.7
  409.5 16.2 collective-permute-done.18
  429.0 19.7 %collective-permute-start.6 = (bf16[256,1536]{1,0:T(8,128)(2,1)}, bf16[256,1536]{1,0:T(8,128)(2,1)}, u32[]{:S(2)}, u32[]{:S(2)}) collective-permute-start(bf16[256,1536]{1,0:T(8,128)(2,1)} %slice.217), channel_id=1, source_target_pairs={{0,3},{1,4},{2,5},{3,6},{4,7},{5,8},{6,9},{7,10},{8,11},{9,12},{10... | collective-permute-start | bytes 2359304 | tf_op jit(solution)/shard_map/ppermute | solution.py:14
  450.8 8.6 collective-permute-done.20
  477.5 8.2 copy.60
  485.8 39.9 %while.131 = (s32[]{:T(128)}, bf16[6,256,128]{1,2,0:T(8,128)(2,1)S(1)}, f32[6,2,256,1]{2,1,3,0:T(2,128)S(1)}, s32[6]{0:T(128)S(1)}, bf16[1792,1536]{0,1:T(8,128)...) while((s32[]{:T(128)}, ...), condition=%wide.region_27.28_spmd.clone, body=%wide.region_24.27_spmd.clone.sunk | while | flops 244088320 | bytes 15100966 | solution.py:128
  540.6 8.7 collective-permute-done.11
  550.2 8.3 copy.56
  559.2 43.4 %while.129 = (s32[]{:T(128)}, bf16[6,256,128]{1,2,0:T(8,128)(2,1)}, f32[6,2,256,1]{2,1,3,0:T(2,128)S(1)}, s32[6]{0:T(128)S(1)}, bf16[1792,1536]{0,1:T(8,128)(2,1...) while((s32[]{:T(128)}, bf16[6,256,128]{1,2,0:T(8,128)(2,1)}, ...), condition=%wide.region_11.12_spmd.clone, body=%wide.region_8.11_spmd.clone.sunk | while | flops 244088320 | bytes 15100966 | solution.py:128
  604.5 9.7 multiply_convert_fusion.6
  618.8 11.6 multiply_convert_fusion.4
  651.3 102.4 %while.132 = (s32[]{:T(128)}, bf16[6,256,128]{1,2,0:T(8,128)(2,1)}, f32[6,1792,128]{1,2,0:T(8,128)}, f32[6,1792,128]{1,2,0:T(8,128)}, s32[6]{0:T(128)S(1)}, /*in...) while((s32[]{:T(128)}, bf16[6,256,128]{1,2,0:T(8,128)(2,1)}, ...), condition=%wide.region_38.39_spmd.clone, body=%wide.region_36.38_spmd.clone.sunk | while | flops 597589504 | bytes 52712600 | solution.py:241
  753.7 7.1 fusion.55
  780.0 6.6 convert_reduce_fusion.1
  786.6 19.6 %collective-permute-done.29 = bf16[256,1536]{0,1:T(8,128)(2,1)S(1)} collective-permute-done((bf16[256,1536]{0,1:T(8,128)(2,1)S(1)}, bf16[256,1536]{0,1:T(8,128)(2,1)S(1)}, u32[]{:S(2)}, u32[]{:S(2)}) %collective-permute-start.29) | collective-permute-done | bytes 786464 | tf_op jit(solution)/shard_map/ppermute | solution.py:14
  811.1 27.0 %collective-permute-done.27 = bf16[256,1536]{0,1:T(8,128)(2,1)S(1)} collective-permute-done((bf16[256,1536]{0,1:T(8,128)(2,1)S(1)}, bf16[256,1536]{0,1:T(8,128)(2,1)S(1)}, u32[]{:S(2)}, u32[]{:S(2)}) %collective-permute-start.27) | collective-permute-done | bytes 786464 | tf_op jit(solution)/shard_map/ppermute | solution.py:14
  863.2 102.2 %while.134 = (s32[]{:T(128)}, bf16[6,256,128]{1,2,0:T(8,128)(2,1)S(1)}, f32[6,1792,128]{1,2,0:T(8,128)}, f32[6,1792,128]{1,2,0:T(8,128)}, s32[6]{0:T(128)S(1)}, ...) while((s32[]{:T(128)}, ...), condition=%wide.region_52.53_spmd.clone, body=%wide.region_50.52_spmd.clone.sunk | while | flops 597589504 | bytes 52712600 | solution.py:241
  965.4 7.2 fusion.53
  980.8 9.7 collective-permute-start.39
  991.8 13.1 collective-permute-start.37
  1012.5 101.9 %while.133 = (s32[]{:T(128)}, bf16[6,256,128]{1,2,0:T(8,128)(2,1)S(1)}, f32[6,1792,128]{1,2,0:T(8,128)}, f32[6,1792,128]{1,2,0:T(8,128)}, s32[6]{0:T(128)S(1)}, ...) while((s32[]{:T(128)}, ...), condition=%wide.region_45.46_spmd.clone, body=%wide.region_43.45_spmd.clone.sunk | while | flops 597589504 | bytes 52712600 | solution.py:241
  1114.4 7.3 fusion.54
  1143.8 14.4 collective-permute-done.36
  1184.3 97.7 %while.135 = (s32[]{:T(128)}, bf16[6,256,128]{1,2,0:T(8,128)(2,1)S(1)}, f32[6,1792,128]{1,2,0:T(8,128)}, f32[6,1792,128]{1,2,0:T(8,128)}, s32[6]{0:T(128)S(1)}, ...) while((s32[]{:T(128)}, ...), condition=%wide.region_59.60_spmd.clone, body=%wide.region_57.59_spmd.clone.sunk | while | flops 597589504 | bytes 52712600 | solution.py:241
  1282.0 7.2 fusion.52
  1295.7 21.4 %collective-permute-start.47 = (bf16[256,1536]{0,1:T(8,128)(2,1)}, bf16[256,1536]{0,1:T(8,128)(2,1)}, u32[]{:S(2)}, u32[]{:S(2)}) collective-permute-start(bf16[256,1536]{0,1:T(8,128)(2,1)} %get-tuple-element.1652), channel_id=1, source_target_pairs={{0,3},{1,4},{2,5},{3,6},{4,7},{5,8},{6,9},{7,10},{8,11},{9,12},{10... | collective-permute-start | bytes 2359304 | tf_op jit(solution)/shard_map/ppermute | solution.py:14
  1323.1 10.8 collective-permute-start.45
  1337.1 40.8 %collective-permute-done.47 = bf16[256,1536]{0,1:T(8,128)(2,1)} collective-permute-done((bf16[256,1536]{0,1:T(8,128)(2,1)}, bf16[256,1536]{0,1:T(8,128)(2,1)}, u32[]{:S(2)}, u32[]{:S(2)}) %collective-permute-start.47) | collective-permute-done | bytes 786464 | tf_op jit(solution)/shard_map/ppermute | solution.py:14
  1384.3 16.5 collective-permute-done.45
  1400.8 10.5 collective-permute-done.43
  1434.8 12.5 add_add_fusion.1
  1460.9 12.9 add_add_fusion
  1483.8 42.1 %all-reduce.22 = (f32[768]{0:T(1024)S(1)}, f32[768]{0:T(1024)S(1)}, f32[768]{0:T(1024)S(1)}, f32[768]{0:T(1024)S(1)}, f32[768]{0:T(1024)S(1)}, /*index=5*/f32[30...) all-reduce(f32[768]{0:T(1024)S(1)} %get-tuple-element.1669, ...), channel_id=3, replica_groups=mesh['dp'=2,'seq'=16] {'dp','seq'}, use_global_device_ids=true, to_apply=%region_65.66.clone | all-reduce | flops 9216 | bytes 73728
  1535.7 39.3 %reduce-scatter.5.cloned.1.call-done = f32[24,2304]{1,0:T(8,128)} async-done(((f32[768,2304]{1,0:T(8,128)}), f32[24,2304]{1,0:T(8,128)}) %reduce-scatter.5.cloned.1.call-update) | async-done | bytes 221200 | tf_op jit(solution)/shard_map/reduce_scatter | solution.py:355
  1575.0 141.4 %reduce-scatter.9.cloned.1.call-done = f32[24,3072]{1,0:T(8,128)} async-done(((f32[768,3072]{1,0:T(8,128)}), f32[24,3072]{1,0:T(8,128)}) %reduce-scatter.9.cloned.1.call-update) | async-done | bytes 294928 | tf_op jit(solution)/shard_map/reduce_scatter | solution.py:362
  1716.4 142.2 %reduce-scatter.11.cloned.1.call-done = f32[96,768]{1,0:T(8,128)} async-done(((f32[3072,768]{1,0:T(8,128)}), f32[96,768]{1,0:T(8,128)}) %reduce-scatter.11.cloned.1.call-update) | async-done | bytes 294928 | tf_op jit(solution)/shard_map/reduce_scatter | solution.py:364
  (1378 shorter events, 857.4 us)
Async XLA Ops:
  7.2 66.7 %all-gather.5.cloned.1.call-start = ((), (), s32[]{:S(2)}) async-start(), calls=%async_computation.4 | async-start | bytes 3649536 | tf_op jit(solution)/shard_map/all_gather | solution.py:329
  7.9 299.0 %all-gather.7.cloned.1.call-start = ((), (), s32[]{:S(2)}) async-start(), calls=%async_computation.5 | async-start | bytes 1216512 | tf_op jit(solution)/shard_map/all_gather | solution.py:332
  8.7 302.5 %all-gather.9.cloned.1.call-start = ((), (), s32[]{:S(2)}) async-start(), calls=%async_computation.6 | async-start | bytes 4866048 | tf_op jit(solution)/shard_map/all_gather | solution.py:336
  9.4 353.5 %all-gather.11.cloned.1.call-start = ((), (), s32[]{:S(2)}) async-start(), calls=%async_computation.7 | async-start | bytes 4866048 | tf_op jit(solution)/shard_map/all_gather | solution.py:338
  10.0 1525.7 %reduce-scatter.7.cloned.1.call-start = ((), (), s32[]{:S(2)}) async-start(), calls=%async_computation.9 | async-start | bytes 2433024 | tf_op jit(solution)/shard_map/reduce_scatter | solution.py:358
  78.0 55.7 %collective-permute-start.12 = (bf16[256,1536]{1,0:T(8,128)(2,1)}, bf16[256,1536]{1,0:T(8,128)(2,1)}, u32[]{:S(2)}, u32[]{:S(2)}) collective-permute-start(bf16[256,1536]{1,0:T(8,128)(2,1)} %slice.218), channel_id=1, source_target_pairs={{0,3},{1,4},{2,5},{3,6},{4,7},{5,8},{6,9},{7,10},{8,11},{9,12},{10... | collective-permute-start | bytes 2359304 | tf_op jit(solution)/shard_map/ppermute | solution.py:14
  82.6 54.6 %collective-permute-start.13 = (bf16[256,1536]{1,0:T(8,128)(2,1)}, bf16[256,1536]{1,0:T(8,128)(2,1)}, u32[]{:S(2)}, u32[]{:S(2)}) collective-permute-start(bf16[256,1536]{1,0:T(8,128)(2,1)} %slice.218), channel_id=1, source_target_pairs={{0,2},{1,3},{2,4},{3,5},{4,6},{5,7},{6,8},{7,9},{8,10},{9,11},{10,... | collective-permute-start | bytes 2359304 | tf_op jit(solution)/shard_map/ppermute | solution.py:14
  87.1 81.4 %collective-permute-start.14 = (bf16[256,1536]{1,0:T(8,128)(2,1)}, bf16[256,1536]{1,0:T(8,128)(2,1)}, u32[]{:S(2)}, u32[]{:S(2)}) collective-permute-start(bf16[256,1536]{1,0:T(8,128)(2,1)} %slice.218), channel_id=1, source_target_pairs={{0,1},{1,2},{2,3},{3,4},{4,5},{5,6},{6,7},{7,8},{8,9},{9,10},{10,1... | collective-permute-start | bytes 2359304 | tf_op jit(solution)/shard_map/ppermute | solution.py:14
  89.6 84.0 %collective-permute-start.15 = (bf16[256,1536]{1,0:T(8,128)(2,1)}, bf16[256,1536]{1,0:T(8,128)(2,1)}, u32[]{:S(2)}, u32[]{:S(2)}) collective-permute-start(bf16[256,1536]{1,0:T(8,128)(2,1)} %slice.218), channel_id=1, source_target_pairs={{1,0},{2,1},{3,2},{4,3},{5,4},{6,5},{7,6},{8,7},{9,8},{10,9},{11,1... | collective-permute-start | bytes 2359304 | tf_op jit(solution)/shard_map/ppermute | solution.py:14
  90.9 89.3 %collective-permute-start.16 = (bf16[256,1536]{1,0:T(8,128)(2,1)}, bf16[256,1536]{1,0:T(8,128)(2,1)}, u32[]{:S(2)}, u32[]{:S(2)}) collective-permute-start(bf16[256,1536]{1,0:T(8,128)(2,1)} %slice.218), channel_id=1, source_target_pairs={{2,0},{3,1},{4,2},{5,3},{6,4},{7,5},{8,6},{9,7},{10,8},{11,9},{12,... | collective-permute-start | bytes 2359304 | tf_op jit(solution)/shard_map/ppermute | solution.py:14
  133.7 49.8 %collective-permute-start.17 = (bf16[256,1536]{1,0:T(8,128)(2,1)}, bf16[256,1536]{1,0:T(8,128)(2,1)S(1)}, u32[]{:S(2)}, u32[]{:S(2)}) collective-permute-start(bf16[256,1536]{1,0:T(8,128)(2,1)} %slice.218), channel_id=1, source_target_pairs={{3,0},{4,1},{5,2},{6,3},{7,4},{8,5},{9,6},{10,7},{11,8},{12,9},{13... | collective-permute-start | bytes 2359304 | tf_op jit(solution)/shard_map/ppermute | solution.py:14
  137.1 96.9 %collective-permute-start = (bf16[256,1536]{1,0:T(8,128)(2,1)}, bf16[256,1536]{1,0:T(8,128)(2,1)}, u32[]{:S(2)}, u32[]{:S(2)}) collective-permute-start(bf16[256,1536]{1,0:T(8,128)(2,1)} %slice.216), channel_id=1, source_target_pairs={{0,3},{1,4},{2,5},{3,6},{4,7},{5,8},{6,9},{7,10},{8,11},{9,12},{10... | collective-permute-start | bytes 2359304 | tf_op jit(solution)/shard_map/ppermute | solution.py:14
  168.5 69.2 %collective-permute-start.1 = (bf16[256,1536]{1,0:T(8,128)(2,1)}, bf16[256,1536]{1,0:T(8,128)(2,1)}, u32[]{:S(2)}, u32[]{:S(2)}) collective-permute-start(bf16[256,1536]{1,0:T(8,128)(2,1)} %slice.216), channel_id=1, source_target_pairs={{0,2},{1,3},{2,4},{3,5},{4,6},{5,7},{6,8},{7,9},{8,10},{9,11},{10,... | collective-permute-start | bytes 2359304 | tf_op jit(solution)/shard_map/ppermute | solution.py:14
  173.7 66.1 %collective-permute-start.2 = (bf16[256,1536]{1,0:T(8,128)(2,1)}, bf16[256,1536]{1,0:T(8,128)(2,1)S(1)}, u32[]{:S(2)}, u32[]{:S(2)}) collective-permute-start(bf16[256,1536]{1,0:T(8,128)(2,1)} %slice.216), channel_id=1, source_target_pairs={{0,1},{1,2},{2,3},{3,4},{4,5},{5,6},{6,7},{7,8},{8,9},{9,10},{10,1... | collective-permute-start | bytes 2359304 | tf_op jit(solution)/shard_map/ppermute | solution.py:14
  180.2 61.5 %collective-permute-start.3 = (bf16[256,1536]{1,0:T(8,128)(2,1)}, bf16[256,1536]{1,0:T(8,128)(2,1)}, u32[]{:S(2)}, u32[]{:S(2)}) collective-permute-start(bf16[256,1536]{1,0:T(8,128)(2,1)} %slice.216), channel_id=1, source_target_pairs={{1,0},{2,1},{3,2},{4,3},{5,4},{6,5},{7,6},{8,7},{9,8},{10,9},{11,1... | collective-permute-start | bytes 2359304 | tf_op jit(solution)/shard_map/ppermute | solution.py:14
  183.6 60.2 %collective-permute-start.4 = (bf16[256,1536]{1,0:T(8,128)(2,1)}, bf16[256,1536]{1,0:T(8,128)(2,1)}, u32[]{:S(2)}, u32[]{:S(2)}) collective-permute-start(bf16[256,1536]{1,0:T(8,128)(2,1)} %slice.216), channel_id=1, source_target_pairs={{2,0},{3,1},{4,2},{5,3},{6,4},{7,5},{8,6},{9,7},{10,8},{11,9},{12,... | collective-permute-start | bytes 2359304 | tf_op jit(solution)/shard_map/ppermute | solution.py:14
  370.9 54.7 %collective-permute-start.18 = (bf16[256,1536]{1,0:T(8,128)(2,1)}, bf16[256,1536]{1,0:T(8,128)(2,1)}, u32[]{:S(2)}, u32[]{:S(2)}) collective-permute-start(bf16[256,1536]{1,0:T(8,128)(2,1)} %slice.219), channel_id=1, source_target_pairs={{0,3},{1,4},{2,5},{3,6},{4,7},{5,8},{6,9},{7,10},{8,11},{9,12},{10... | collective-permute-start | bytes 2359304 | tf_op jit(solution)/shard_map/ppermute | solution.py:14
  375.3 53.7 %collective-permute-start.19 = (bf16[256,1536]{1,0:T(8,128)(2,1)}, bf16[256,1536]{1,0:T(8,128)(2,1)}, u32[]{:S(2)}, u32[]{:S(2)}) collective-permute-start(bf16[256,1536]{1,0:T(8,128)(2,1)} %slice.219), channel_id=1, source_target_pairs={{0,2},{1,3},{2,4},{3,5},{4,6},{5,7},{6,8},{7,9},{8,10},{9,11},{10,... | collective-permute-start | bytes 2359304 | tf_op jit(solution)/shard_map/ppermute | solution.py:14
  380.9 78.5 %collective-permute-start.20 = (bf16[256,1536]{1,0:T(8,128)(2,1)}, bf16[256,1536]{1,0:T(8,128)(2,1)}, u32[]{:S(2)}, u32[]{:S(2)}) collective-permute-start(bf16[256,1536]{1,0:T(8,128)(2,1)} %slice.219), channel_id=1, source_target_pairs={{0,1},{1,2},{2,3},{3,4},{4,5},{5,6},{6,7},{7,8},{8,9},{9,10},{10,1... | collective-permute-start | bytes 2359304 | tf_op jit(solution)/shard_map/ppermute | solution.py:14
  383.8 80.8 %collective-permute-start.21 = (bf16[256,1536]{1,0:T(8,128)(2,1)}, bf16[256,1536]{1,0:T(8,128)(2,1)}, u32[]{:S(2)}, u32[]{:S(2)}) collective-permute-start(bf16[256,1536]{1,0:T(8,128)(2,1)} %slice.219), channel_id=1, source_target_pairs={{1,0},{2,1},{3,2},{4,3},{5,4},{6,5},{7,6},{8,7},{9,8},{10,9},{11,1... | collective-permute-start | bytes 2359304 | tf_op jit(solution)/shard_map/ppermute | solution.py:14
  385.1 86.9 %collective-permute-start.22 = (bf16[256,1536]{1,0:T(8,128)(2,1)}, bf16[256,1536]{1,0:T(8,128)(2,1)}, u32[]{:S(2)}, u32[]{:S(2)}) collective-permute-start(bf16[256,1536]{1,0:T(8,128)(2,1)} %slice.219), channel_id=1, source_target_pairs={{2,0},{3,1},{4,2},{5,3},{6,4},{7,5},{8,6},{9,7},{10,8},{11,9},{12,... | collective-permute-start | bytes 2359304 | tf_op jit(solution)/shard_map/ppermute | solution.py:14
  425.6 49.7 %collective-permute-start.23 = (bf16[256,1536]{1,0:T(8,128)(2,1)}, bf16[256,1536]{1,0:T(8,128)(2,1)S(1)}, u32[]{:S(2)}, u32[]{:S(2)}) collective-permute-start(bf16[256,1536]{1,0:T(8,128)(2,1)} %slice.219), channel_id=1, source_target_pairs={{3,0},{4,1},{5,2},{6,3},{7,4},{8,5},{9,6},{10,7},{11,8},{12,9},{13... | collective-permute-start | bytes 2359304 | tf_op jit(solution)/shard_map/ppermute | solution.py:14
  429.0 96.7 %collective-permute-start.6 = (bf16[256,1536]{1,0:T(8,128)(2,1)}, bf16[256,1536]{1,0:T(8,128)(2,1)}, u32[]{:S(2)}, u32[]{:S(2)}) collective-permute-start(bf16[256,1536]{1,0:T(8,128)(2,1)} %slice.217), channel_id=1, source_target_pairs={{0,3},{1,4},{2,5},{3,6},{4,7},{5,8},{6,9},{7,10},{8,11},{9,12},{10... | collective-permute-start | bytes 2359304 | tf_op jit(solution)/shard_map/ppermute | solution.py:14
  459.3 70.1 %collective-permute-start.7 = (bf16[256,1536]{1,0:T(8,128)(2,1)}, bf16[256,1536]{1,0:T(8,128)(2,1)}, u32[]{:S(2)}, u32[]{:S(2)}) collective-permute-start(bf16[256,1536]{1,0:T(8,128)(2,1)} %slice.217), channel_id=1, source_target_pairs={{0,2},{1,3},{2,4},{3,5},{4,6},{5,7},{6,8},{7,9},{8,10},{9,11},{10,... | collective-permute-start | bytes 2359304 | tf_op jit(solution)/shard_map/ppermute | solution.py:14
  464.5 67.0 %collective-permute-start.8 = (bf16[256,1536]{1,0:T(8,128)(2,1)}, bf16[256,1536]{1,0:T(8,128)(2,1)}, u32[]{:S(2)}, u32[]{:S(2)}) collective-permute-start(bf16[256,1536]{1,0:T(8,128)(2,1)} %slice.217), channel_id=1, source_target_pairs={{0,1},{1,2},{2,3},{3,4},{4,5},{5,6},{6,7},{7,8},{8,9},{9,10},{10,1... | collective-permute-start | bytes 2359304 | tf_op jit(solution)/shard_map/ppermute | solution.py:14
  471.9 64.5 %collective-permute-start.9 = (bf16[256,1536]{1,0:T(8,128)(2,1)}, bf16[256,1536]{1,0:T(8,128)(2,1)}, u32[]{:S(2)}, u32[]{:S(2)}) collective-permute-start(bf16[256,1536]{1,0:T(8,128)(2,1)} %slice.217), channel_id=1, source_target_pairs={{1,0},{2,1},{3,2},{4,3},{5,4},{6,5},{7,6},{8,7},{9,8},{10,9},{11,1... | collective-permute-start | bytes 2359304 | tf_op jit(solution)/shard_map/ppermute | solution.py:14
  475.3 63.2 %collective-permute-start.10 = (bf16[256,1536]{1,0:T(8,128)(2,1)}, bf16[256,1536]{1,0:T(8,128)(2,1)}, u32[]{:S(2)}, u32[]{:S(2)}) collective-permute-start(bf16[256,1536]{1,0:T(8,128)(2,1)} %slice.217), channel_id=1, source_target_pairs={{2,0},{3,1},{4,2},{5,3},{6,4},{7,5},{8,6},{9,7},{10,8},{11,9},{12,... | collective-permute-start | bytes 2359304 | tf_op jit(solution)/shard_map/ppermute | solution.py:14
  769.6 68.5 %collective-permute-start.27 = (bf16[256,1536]{0,1:T(8,128)(2,1)S(1)}, bf16[256,1536]{0,1:T(8,128)(2,1)S(1)}, u32[]{:S(2)}, u32[]{:S(2)}) collective-permute-start(bf16[256,1536]{0,1:T(8,128)(2,1)S(1)} %get-tuple-element.1648), channel_id=1, source_target_pairs={{0,2},{1,3},{2,4},{3,5},{4,6},{5,7},{6,8},{7,9},{8,10},{9,11},{10,... | collective-permute-start | bytes 2359304 | tf_op jit(solution)/shard_map/ppermute | solution.py:14
  774.2 63.9 %collective-permute-start.26 = (bf16[256,1536]{0,1:T(8,128)(2,1)S(1)}, bf16[256,1536]{0,1:T(8,128)(2,1)S(1)}, u32[]{:S(2)}, u32[]{:S(2)}) collective-permute-start(bf16[256,1536]{0,1:T(8,128)(2,1)S(1)} %get-tuple-element.1649), channel_id=1, source_target_pairs={{2,0},{3,1},{4,2},{5,3},{6,4},{7,5},{8,6},{9,7},{10,8},{11,9},{12,... | collective-permute-start | bytes 2359304 | tf_op jit(solution)/shard_map/ppermute | solution.py:14
  775.5 62.6 %collective-permute-start.25 = (bf16[256,1536]{0,1:T(8,128)(2,1)S(1)}, bf16[256,1536]{0,1:T(8,128)(2,1)S(1)}, u32[]{:S(2)}, u32[]{:S(2)}) collective-permute-start(bf16[256,1536]{0,1:T(8,128)(2,1)S(1)} %get-tuple-element.1650), channel_id=1, source_target_pairs={{0,1},{1,2},{2,3},{3,4},{4,5},{5,6},{6,7},{7,8},{8,9},{9,10},{10,1... | collective-permute-start | bytes 2359304 | tf_op jit(solution)/shard_map/ppermute | solution.py:14
  977.3 144.4 %collective-permute-start.41 = (bf16[256,1536]{0,1:T(8,128)(2,1)}, bf16[256,1536]{0,1:T(8,128)(2,1)}, u32[]{:S(2)}, u32[]{:S(2)}) collective-permute-start(bf16[256,1536]{0,1:T(8,128)(2,1)} %get-tuple-element.1658), channel_id=1, source_target_pairs={{0,3},{1,4},{2,5},{3,6},{4,7},{5,8},{6,9},{7,10},{8,11},{9,12},{10... | collective-permute-start | bytes 2359304 | tf_op jit(solution)/shard_map/ppermute | solution.py:14
  979.5 150.8 %collective-permute-start.40 = (bf16[256,1536]{0,1:T(8,128)(2,1)}, bf16[256,1536]{0,1:T(8,128)(2,1)}, u32[]{:S(2)}, u32[]{:S(2)}) collective-permute-start(bf16[256,1536]{0,1:T(8,128)(2,1)} %get-tuple-element.1659), channel_id=1, source_target_pairs={{3,0},{4,1},{5,2},{6,3},{7,4},{8,5},{9,6},{10,7},{11,8},{12,9},{13... | collective-permute-start | bytes 2359304 | tf_op jit(solution)/shard_map/ppermute | solution.py:14
  980.8 156.1 %collective-permute-start.39 = (bf16[256,1536]{0,1:T(8,128)(2,1)}, bf16[256,1536]{0,1:T(8,128)(2,1)}, u32[]{:S(2)}, u32[]{:S(2)}) collective-permute-start(bf16[256,1536]{0,1:T(8,128)(2,1)} %get-tuple-element.1660), channel_id=1, source_target_pairs={{0,2},{1,3},{2,4},{3,5},{4,6},{5,7},{6,8},{7,9},{8,10},{9,11},{10,... | collective-permute-start | bytes 2359304 | tf_op jit(solution)/shard_map/ppermute | solution.py:14
  990.5 147.7 %collective-permute-start.38 = (bf16[256,1536]{0,1:T(8,128)(2,1)}, bf16[256,1536]{0,1:T(8,128)(2,1)}, u32[]{:S(2)}, u32[]{:S(2)}) collective-permute-start(bf16[256,1536]{0,1:T(8,128)(2,1)} %get-tuple-element.1661), channel_id=1, source_target_pairs={{2,0},{3,1},{4,2},{5,3},{6,4},{7,5},{8,6},{9,7},{10,8},{11,9},{12,... | collective-permute-start | bytes 2359304 | tf_op jit(solution)/shard_map/ppermute | solution.py:14
  991.8 150.8 %collective-permute-start.37 = (bf16[256,1536]{0,1:T(8,128)(2,1)}, bf16[256,1536]{0,1:T(8,128)(2,1)}, u32[]{:S(2)}, u32[]{:S(2)}) collective-permute-start(bf16[256,1536]{0,1:T(8,128)(2,1)} %get-tuple-element.1662), channel_id=1, source_target_pairs={{0,1},{1,2},{2,3},{3,4},{4,5},{5,6},{6,7},{7,8},{8,9},{9,10},{10,1... | collective-permute-start | bytes 2359304 | tf_op jit(solution)/shard_map/ppermute | solution.py:14
  1130.3 163.9 %collective-permute-start.35 = (bf16[256,1536]{0,1:T(8,128)(2,1)}, bf16[256,1536]{0,1:T(8,128)(2,1)}, u32[]{:S(2)}, u32[]{:S(2)}) collective-permute-start(bf16[256,1536]{0,1:T(8,128)(2,1)} %get-tuple-element.1640), channel_id=1, source_target_pairs={{0,3},{1,4},{2,5},{3,6},{4,7},{5,8},{6,9},{7,10},{8,11},{9,12},{10... | collective-permute-start | bytes 2359304 | tf_op jit(solution)/shard_map/ppermute | solution.py:14
  1136.9 158.7 %collective-permute-start.34 = (bf16[256,1536]{0,1:T(8,128)(2,1)}, bf16[256,1536]{0,1:T(8,128)(2,1)}, u32[]{:S(2)}, u32[]{:S(2)}) collective-permute-start(bf16[256,1536]{0,1:T(8,128)(2,1)} %get-tuple-element.1641), channel_id=1, source_target_pairs={{3,0},{4,1},{5,2},{6,3},{7,4},{8,5},{9,6},{10,7},{11,8},{12,9},{13... | collective-permute-start | bytes 2359304 | tf_op jit(solution)/shard_map/ppermute | solution.py:14
  1138.2 183.6 %collective-permute-start.33 = (bf16[256,1536]{0,1:T(8,128)(2,1)}, bf16[256,1536]{0,1:T(8,128)(2,1)}, u32[]{:S(2)}, u32[]{:S(2)}) collective-permute-start(bf16[256,1536]{0,1:T(8,128)(2,1)} %get-tuple-element.1642), channel_id=1, source_target_pairs={{0,2},{1,3},{2,4},{3,5},{4,6},{5,7},{6,8},{7,9},{8,10},{9,11},{10,... | collective-permute-start | bytes 2359304 | tf_op jit(solution)/shard_map/ppermute | solution.py:14
  1142.5 180.6 %collective-permute-start.32 = (bf16[256,1536]{0,1:T(8,128)(2,1)}, bf16[256,1536]{0,1:T(8,128)(2,1)}, u32[]{:S(2)}, u32[]{:S(2)}) collective-permute-start(bf16[256,1536]{0,1:T(8,128)(2,1)} %get-tuple-element.1643), channel_id=1, source_target_pairs={{2,0},{3,1},{4,2},{5,3},{6,4},{7,5},{8,6},{9,7},{10,8},{11,9},{12,... | collective-permute-start | bytes 2359304 | tf_op jit(solution)/shard_map/ppermute | solution.py:14
  1158.2 175.7 %collective-permute-start.31 = (bf16[256,1536]{0,1:T(8,128)(2,1)}, bf16[256,1536]{0,1:T(8,128)(2,1)}, u32[]{:S(2)}, u32[]{:S(2)}) collective-permute-start(bf16[256,1536]{0,1:T(8,128)(2,1)} %get-tuple-element.1644), channel_id=1, source_target_pairs={{0,1},{1,2},{2,3},{3,4},{4,5},{5,6},{6,7},{7,8},{8,9},{9,10},{10,1... | collective-permute-start | bytes 2359304 | tf_op jit(solution)/shard_map/ppermute | solution.py:14
  1295.7 82.3 %collective-permute-start.47 = (bf16[256,1536]{0,1:T(8,128)(2,1)}, bf16[256,1536]{0,1:T(8,128)(2,1)}, u32[]{:S(2)}, u32[]{:S(2)}) collective-permute-start(bf16[256,1536]{0,1:T(8,128)(2,1)} %get-tuple-element.1652), channel_id=1, source_target_pairs={{0,3},{1,4},{2,5},{3,6},{4,7},{5,8},{6,9},{7,10},{8,11},{9,12},{10... | collective-permute-start | bytes 2359304 | tf_op jit(solution)/shard_map/ppermute | solution.py:14
  1319.1 255.9 %reduce-scatter.5.cloned.1.call-start = ((), (), s32[]{:S(2)}) async-start(), calls=%async_computation.8 | async-start | bytes 7299072 | tf_op jit(solution)/shard_map/reduce_scatter | solution.py:355
  1321.8 62.5 %collective-permute-start.46 = (bf16[256,1536]{0,1:T(8,128)(2,1)S(1)}, bf16[256,1536]{0,1:T(8,128)(2,1)S(1)}, u32[]{:S(2)}, u32[]{:S(2)}) collective-permute-start(bf16[256,1536]{0,1:T(8,128)(2,1)S(1)} %copy-done.101), channel_id=1, source_target_pairs={{3,0},{4,1},{5,2},{6,3},{7,4},{8,5},{9,6},{10,7},{11,8},{12,9},{13... | collective-permute-start | bytes 2359304 | tf_op jit(solution)/shard_map/ppermute | solution.py:14
  1323.1 77.6 %collective-permute-start.45 = (bf16[256,1536]{0,1:T(8,128)(2,1)S(1)}, bf16[256,1536]{0,1:T(8,128)(2,1)S(1)}, u32[]{:S(2)}, u32[]{:S(2)}) collective-permute-start(bf16[256,1536]{0,1:T(8,128)(2,1)S(1)} %copy-done.100), channel_id=1, source_target_pairs={{0,2},{1,3},{2,4},{3,5},{4,6},{5,7},{6,8},{7,9},{8,10},{9,11},{10,... | collective-permute-start | bytes 2359304 | tf_op jit(solution)/shard_map/ppermute | solution.py:14
  1334.0 66.8 %collective-permute-start.44 = (bf16[256,1536]{0,1:T(8,128)(2,1)S(1)}, bf16[256,1536]{0,1:T(8,128)(2,1)S(1)}, u32[]{:S(2)}, u32[]{:S(2)}) collective-permute-start(bf16[256,1536]{0,1:T(8,128)(2,1)S(1)} %copy-done.99), channel_id=1, source_target_pairs={{2,0},{3,1},{4,2},{5,3},{6,4},{7,5},{8,6},{9,7},{10,8},{11,9},{12,... | collective-permute-start | bytes 2359304 | tf_op jit(solution)/shard_map/ppermute | solution.py:14
  1335.3 75.9 %collective-permute-start.43 = (bf16[256,1536]{0,1:T(8,128)(2,1)S(1)}, bf16[256,1536]{0,1:T(8,128)(2,1)S(1)}, u32[]{:S(2)}, u32[]{:S(2)}) collective-permute-start(bf16[256,1536]{0,1:T(8,128)(2,1)S(1)} %copy-done.98), channel_id=1, source_target_pairs={{0,1},{1,2},{2,3},{3,4},{4,5},{5,6},{6,7},{7,8},{8,9},{9,10},{10,1... | collective-permute-start | bytes 2359304 | tf_op jit(solution)/shard_map/ppermute | solution.py:14
  1420.1 296.3 %reduce-scatter.9.cloned.1.call-start = ((), (), s32[]{:S(2)}) async-start(), calls=%async_computation.10 | async-start | bytes 9732096 | tf_op jit(solution)/shard_map/reduce_scatter | solution.py:362
  1447.4 411.1 %reduce-scatter.11.cloned.1.call-start = ((), (), s32[]{:S(2)}) async-start(), calls=%async_computation.11 | async-start | bytes 9732096 | tf_op jit(solution)/shard_map/reduce_scatter | solution.py:364
  (240 other events, 6319.4 us)
Sparse Core Ops, SparseCore 0:
  10.9 62.9 all-gather.4
  76.7 124.6 all-gather.6
  204.3 93.2 all-gather.8
  300.4 62.4 all-gather.10
  1319.2 129.9 reduce-scatter.6
  1456.2 118.7 reduce-scatter.4
  1581.4 134.8 reduce-scatter.8
  1723.8 134.6 reduce-scatter.10
where the time goes:
time: 1880 us; the launch traced here: 1870 us
  waiting for transfers between devices  597 us (32%)
  matrix products  406 us (22%)
  local copies, waits for them, and re-layouts  362 us (19%)
  starting transfers between devices  199 us (11%)
  other arithmetic  117 us (6%)
  blocking collectives  84.5 us (4%)
  loops' own time  81.6 us (4%)
    ppermute x48, waiting for transfers between devices, from_behind(): return lax.ppermute(block, axis, route)  220 us
    ppermute x48, starting transfers between devices, from_behind(): return lax.ppermute(block, axis, route)  199 us
    reduce_scatter x1, waiting for transfers between devices, per_device(): lax.psum_scatter(totals[9], ('dp', 'seq'), scatter_dimension=0, tiled=True)  142 us
    reduce_scatter x1, waiting for transfers between devices, per_device(): lax.psum_scatter(totals[7], ('dp', 'seq'), scatter_dimension=0, tiled=True)  141 us
    unnamed x475, local copies, waits for them, and re-layouts  107 us
    dot_general x48, matrix products, score_block(): jnp.einsum('qhd,khd->hqk', queries, keys_grp, preferred_element_type=jnp....  92.7 us
    unnamed x2, blocking collectives  84.5 us
    dot_general x24, matrix products, attend_back(): jnp.einsum('qhd,khd->hqk', grad_ctx, values_grp, preferred_element_type=j...  70.7 us
  transfers between devices with their start and end apart: 56, of which 18 were waited for; matrix products, arithmetic and copies ran while one was open for 30% of the time, Pallas kernels for 0%

commit v1 on v0

v1 whole, which is shorter than its diff:
```python
import functools

import jax
import jax.numpy as jnp
from jax import lax
from jax.experimental import pallas as pl
from jax.experimental.pallas import tpu as pltpu
from jax.sharding import PartitionSpec as P

HEADS = 12
HEAD = 64
PAIR = 2 * HEAD
REACH = 3
TILE = 256
LINE = 4

F32 = jnp.float32
BF16 = jnp.bfloat16


def pick_lanes(block, half):
    lanes = lax.broadcasted_iota(jnp.int32, block.shape, 1)
    keep = (lanes < HEAD) if half == 0 else (lanes >= HEAD)
    return jnp.where(keep, block, jnp.zeros_like(block))


def dot_nt(left, right):
    return lax.dot_general(left, right, (((1,), (1,)), ((), ())), preferred_element_type=F32)


def dot_tn(left, right):
    return lax.dot_general(left, right, (((0,), (0,)), ((), ())), preferred_element_type=F32)


def dot_nn(left, right):
    return lax.dot_general(left, right, (((1,), (0,)), ((), ())), preferred_element_type=F32)


def attend_kernel(span, q_ref, k_ref, v_ref, segq, segk, padk, ctx_ref, lse_ref, bias, scores):
    pair = pl.program_id(0)
    rows = q_ref.shape[0]
    window = k_ref.shape[0]
    tiles = rows // TILE
    for tile in range(tiles):
        at = slice(tile * TILE, (tile + 1) * TILE)
        low, high = span[tile, 0], span[tile, 1]

        @pl.when(pair == 0)
        def _():
            def fill(block, carry):
                cols = pl.ds(pl.multiple_of(block * TILE, TILE), TILE)
                row_at = lax.broadcasted_iota(jnp.int32, (TILE, TILE), 0) + (REACH * TILE + tile * TILE)
                col_at = lax.broadcasted_iota(jnp.int32, (TILE, TILE), 1) + block * TILE
                same = segq[at, :] == segk[:, cols]
                open_key = (padk[:, cols] == 1) | (row_at == col_at)
                bias[at, cols] = jnp.where(same & open_key, 0.0, -1e30)
                return carry
            lax.fori_loop(low, high, fill, 0)

        query = q_ref[at, :]
        halves = [pick_lanes(query, half) for half in range(2)]
        start = jnp.full((TILE, 128), -3e38, F32)

        def first(block, tops):
            cols = pl.ds(pl.multiple_of(block * TILE, TILE), TILE)
            keys = k_ref[cols, :]
            shade = bias[at, cols]
            out = []
            for half in range(2):
                part = dot_nt(halves[half], keys) + shade
                scores[half, :, cols] = part
                out.append(jnp.maximum(tops[half], jnp.maximum(part[:, :128], part[:, 128:])))
            return tuple(out)

        tops = lax.fori_loop(low, high, first, (start, start))
        tops = [jnp.max(top, axis=1, keepdims=True) for top in tops]

        def second(block, carry):
            cols = pl.ds(pl.multiple_of(block * TILE, TILE), TILE)
            values = v_ref[cols, :]
            out = []
            for half in range(2):
                total, acc = carry[2 * half], carry[2 * half + 1]
                probs = jnp.exp(scores[half, :, cols] - tops[half])
                total = total + (probs[:, :128] + probs[:, 128:])
                acc = acc + dot_nn(probs.astype(BF16), values)
                out += [total, acc]
            return tuple(out)

        zero = jnp.zeros((TILE, 128), F32)
        parts = lax.fori_loop(low, high, second, (zero,) * 4)
        done = []
        for half in range(2):
            total = jnp.sum(parts[2 * half], axis=1, keepdims=True)
            done.append(parts[2 * half + 1] / total)
            column = tops[half] + jnp.log(total)
            flat = jnp.transpose(jnp.broadcast_to(column, (TILE, 128)))
            lse_ref[0, half : half + 1, at] = flat[0:1, :]
        lanes = lax.broadcasted_iota(jnp.int32, (TILE, PAIR), 1)
        ctx_ref[at, :] = jnp.where(lanes < HEAD, done[0], done[1]).astype(BF16)


def attend(q, kv, span, segq, segk, padk):
    rows, width = q.shape
    window = kv.shape[0]
    pairs = width // PAIR
    whole = lambda shape: pl.BlockSpec(shape, lambda p, s: (0,) * len(shape))
    return pl.pallas_call(
        attend_kernel,
        grid_spec=pltpu.PrefetchScalarGridSpec(
            num_scalar_prefetch=1,
            grid=(pairs,),
            in_specs=[
                pl.BlockSpec((rows, PAIR), lambda p, s: (0, p)),
                pl.BlockSpec((window, PAIR), lambda p, s: (0, p)),
                pl.BlockSpec((window, PAIR), lambda p, s: (0, pairs + p)),
                whole((rows, 1)),
                whole((1, window)),
                whole((1, window)),
            ],
            out_specs=[
                pl.BlockSpec((rows, PAIR), lambda p, s: (0, p)),
                pl.BlockSpec((1, 8, rows), lambda p, s: (p, 0, 0)),
            ],
            scratch_shapes=[
                pltpu.VMEM((rows, window), F32),
                pltpu.VMEM((2, TILE, window), F32),
            ],
        ),
        out_shape=[
            jax.ShapeDtypeStruct((rows, width), BF16),
            jax.ShapeDtypeStruct((pairs, 8, rows), F32),
        ],
        name="attend",
    )(span, q, kv, kv, segq, segk, padk)


def attend_back_kernel(
    span, q_ref, k_ref, v_ref, dc_ref, lse_ref, segq, segk, padk, dq_ref, dk_ref, dv_ref, bias, dk_acc, dv_acc, keep_p, keep_d
):
    pair = pl.program_id(0)
    rows = q_ref.shape[0]
    window = k_ref.shape[0]
    tiles = rows // TILE
    dk_acc[...] = jnp.zeros_like(dk_acc)
    dv_acc[...] = jnp.zeros_like(dv_acc)
    for tile in range(tiles):
        at = slice(tile * TILE, (tile + 1) * TILE)
        low, high = span[tile, 0], span[tile, 1]

        @pl.when(pair == 0)
        def _():
            def fill(block, carry):
                keys = pl.ds(pl.multiple_of(block * TILE, TILE), TILE)
                key_at = lax.broadcasted_iota(jnp.int32, (TILE, TILE), 0) + block * TILE
                row_at = lax.broadcasted_iota(jnp.int32, (TILE, TILE), 1) + (REACH * TILE + tile * TILE)
                same = segk[keys, :] == segq[:, at]
                open_key = (padk[keys, :] == 1) | (row_at == key_at)
                bias[keys, at] = jnp.where(same & open_key, 0.0, -1e30)
                return carry
            lax.fori_loop(low, high, fill, 0)

        query = q_ref[at, :]
        dctx = dc_ref[at, :]
        q_half = [pick_lanes(query, half) for half in range(2)]
        c_half = [pick_lanes(dctx, half) for half in range(2)]

        zero = jnp.zeros((8, TILE), F32)

        def first(block, inner):
            keys = pl.ds(pl.multiple_of(block * TILE, TILE), TILE)
            key = k_ref[keys, :]
            value = v_ref[keys, :]
            shade = bias[keys, at]
            add_v = jnp.zeros((TILE, PAIR), F32)
            out = []
            for half in range(2):
                part = dot_nt(key, q_half[half]) + shade
                probs = jnp.exp(part - lse_ref[0, half : half + 1, at])
                dprobs = dot_nt(value, c_half[half])
                add_v = add_v + dot_nn(probs.astype(BF16), c_half[half])
                keep_p[half, keys, :] = probs
                keep_d[half, keys, :] = dprobs
                out.append(inner[half] + jnp.sum((probs * dprobs).reshape(TILE // 8, 8, TILE), axis=0))
            dv_acc[keys, :] += add_v
            return tuple(out)

        inner = lax.fori_loop(low, high, first, (zero, zero))
        inner = [jnp.sum(item, axis=0, keepdims=True) for item in inner]

        def second(block, dq):
            keys = pl.ds(pl.multiple_of(block * TILE, TILE), TILE)
            key = k_ref[keys, :]
            add_k = jnp.zeros((TILE, PAIR), F32)
            for half in range(2):
                dscore = (keep_p[half, keys, :] * (keep_d[half, keys, :] - inner[half])).astype(BF16)
                add_k = add_k + dot_nn(dscore, q_half[half])
                dq = dq + dot_tn(dscore, pick_lanes(key, half))
            dk_acc[keys, :] += add_k
            return dq

        dq = lax.fori_loop(low, high, second, jnp.zeros((TILE, PAIR), F32))
        dq_ref[at, :] = (dq * 0.125).astype(BF16)
    dk_ref[...] = dk_acc[...].astype(BF16)
    dv_ref[...] = dv_acc[...].astype(BF16)


def attend_back(q, kv, dctx, lse, span, segq, segk, padk):
    rows, width = q.shape
    window = kv.shape[0]
    pairs = width // PAIR
    whole = lambda shape: pl.BlockSpec(shape, lambda p, s: (0,) * len(shape))
    return pl.pallas_call(
        attend_back_kernel,
        grid_spec=pltpu.PrefetchScalarGridSpec(
            num_scalar_prefetch=1,
            grid=(pairs,),
            in_specs=[
                pl.BlockSpec((rows, PAIR), lambda p, s: (0, p)),
                pl.BlockSpec((window, PAIR), lambda p, s: (0, p)),
                pl.BlockSpec((window, PAIR), lambda p, s: (0, pairs + p)),
                pl.BlockSpec((rows, PAIR), lambda p, s: (0, p)),
                pl.BlockSpec((1, 8, rows), lambda p, s: (p, 0, 0)),
                whole((1, rows)),
                whole((window, 1)),
                whole((window, 1)),
            ],
            out_specs=[
                pl.BlockSpec((rows, PAIR), lambda p, s: (0, p)),
                pl.BlockSpec((window, PAIR), lambda p, s: (0, p)),
                pl.BlockSpec((window, PAIR), lambda p, s: (0, p)),
            ],
            scratch_shapes=[
                pltpu.VMEM((window, rows), F32),
                pltpu.VMEM((window, PAIR), F32),
                pltpu.VMEM((window, PAIR), F32),
                pltpu.VMEM((2, window, TILE), F32),
                pltpu.VMEM((2, window, TILE), F32),
            ],
        ),
        out_shape=[
            jax.ShapeDtypeStruct((rows, width), BF16),
            jax.ShapeDtypeStruct((window, width), BF16),
            jax.ShapeDtypeStruct((window, width), BF16),
        ],
        name="attend_back",
    )(span, q, kv, kv, dctx, lse, segq, segk, padk)


def norm_stats(resid):
    center = resid - jnp.mean(resid, axis=-1, keepdims=True)
    spread = jnp.mean(center * center, axis=-1, keepdims=True)
    scale = lax.rsqrt(spread + 1e-12)
    return center * scale, scale


def norm_back(grad, resid, gain):
    unit, scale = norm_stats(resid)
    inner = grad * gain
    back = scale * (
        inner - jnp.mean(inner, axis=-1, keepdims=True) - unit * jnp.mean(inner * unit, axis=-1, keepdims=True)
    )
    return back, jnp.sum(grad * unit, axis=0), jnp.sum(grad, axis=0)


class Place:
    def __init__(self):
        self.size = lax.axis_size("seq")
        self.seq = lax.axis_index("seq")
        self.core = lax.axis_index("dp")

    def flat(self, core, seq):
        return core * self.size + seq

    def move(self, block, delta):
        pairs = []
        for seq in range(self.size):
            for core in range(2):
                unit = 2 * (seq // LINE) + core + delta
                if 0 <= unit < 2 * (self.size // LINE):
                    pairs.append((self.flat(core, seq), self.flat(unit % 2, (unit // 2) * LINE + seq % LINE)))
        return lax.ppermute(block, ("dp", "seq"), pairs)

    def route(self, turn, back=False):
        pairs = []
        for seq in range(self.size):
            for core in range(2):
                spot = seq % LINE
                row = turn if seq % 2 == 0 else 1 - turn
                goal = self.flat(spot // 2, (seq // LINE) * LINE + 2 * core + row)
                pairs.append((self.flat(core, seq), goal))
        return [(b, a) for a, b in pairs] if back else pairs

    def take_in(self, both):
        even = self.seq % 2 == 0
        send = [jnp.where(even, both[t], both[1 - t]) for t in range(2)]
        got = [lax.ppermute(send[t], ("dp", "seq"), self.route(t)) for t in range(2)]
        odd_line = self.seq % 2 == 1
        first = jnp.where(odd_line, got[1], got[0])
        last = jnp.where(odd_line, got[0], got[1])
        return jnp.concatenate([first, last], axis=0)

    def give_back(self, own):
        half = own.shape[0] // 2
        first, last = own[:half], own[half:]
        odd_line = self.seq % 2 == 1
        send = [jnp.where(odd_line, last, first), jnp.where(odd_line, first, last)]
        got = [lax.ppermute(send[t], ("dp", "seq"), self.route(t, True)) for t in range(2)]
        even = self.seq % 2 == 0
        return jnp.stack([jnp.where(even, got[0], got[1]), jnp.where(even, got[1], got[0])])

    def widen(self, own):
        half = own.shape[0] // 2
        return jnp.concatenate(
            [self.move(own[half:], 2), self.move(own, 1), own, self.move(own, -1), self.move(own[:half], -2)], axis=0
        )

    def narrow(self, wide):
        half = wide.shape[0] // 8
        own = wide[3 * half : 5 * half]
        low = wide.astype(BF16)
        own = own + self.move(low[half : 3 * half], -1).astype(F32) + self.move(low[5 * half : 7 * half], 1).astype(F32)
        top = self.move(low[7 * half :], 2).astype(F32)
        bottom = self.move(low[:half], -2).astype(F32)
        return own + jnp.concatenate([top, bottom], axis=0)


def forward_layer(wide, state, full, marks):
    rows = state.shape[0]
    width = state.shape[1]
    w_qkv, b_q, b_v, w_out, b_out, gain1, shift1, w_up, b_up, w_down, b_down, gain2, shift2 = full
    span, segq, segk, padk = marks
    own = state.astype(BF16)
    q = ((dot_nn(own, w_qkv[:, :width]) + b_q) * 0.125).astype(BF16)
    bias = jnp.concatenate([jnp.zeros_like(b_v), b_v])
    kv = (dot_nn(wide, w_qkv[:, width:]) + bias).astype(BF16)
    ctx, lse = attend(q, kv, span, segq[:, None], segk[None], padk[None])
    resid1 = state + dot_nn(ctx, w_out) + b_out
    unit, _ = norm_stats(resid1)
    hidden = unit * gain1 + shift1
    hidden_low = hidden.astype(BF16)
    up = dot_nn(hidden_low, w_up) + b_up
    active = (up * (0.5 * (1.0 + lax.erf(up * (2.0**-0.5))))).astype(BF16)
    resid2 = hidden + dot_nn(active, w_down) + b_down
    unit, _ = norm_stats(resid2)
    result = unit * gain2 + shift2
    return result, (own, wide, q, kv, ctx, lse, resid1, hidden_low, up, active, resid2)


def backward_layer(grad, full, saved, marks):
    w_qkv, b_q, b_v, w_out, b_out, gain1, shift1, w_up, b_up, w_down, b_down, gain2, shift2 = full
    span, segq, segk, padk = marks
    own, wide, q, kv, ctx, lse, resid1, hidden_low, up, active, resid2 = saved
    rows, width = resid1.shape
    grad2, g_gain2, g_shift2 = norm_back(grad, resid2, gain2)
    d_ffn = grad2.astype(BF16)
    g_bdown = jnp.sum(d_ffn.astype(F32), axis=0)
    g_wdown = dot_tn(active, d_ffn)
    d_active = dot_nt(d_ffn, w_down)
    slope = 0.5 * (1.0 + lax.erf(up * (2.0**-0.5))) + up * jnp.exp(-0.5 * up * up) * 0.3989422804014327
    d_up = (d_active * slope).astype(BF16)
    g_wup = dot_tn(hidden_low, d_up)
    g_bup = jnp.sum(d_up.astype(F32), axis=0)
    d_hidden = grad2 + dot_nt(d_up, w_up)
    grad1, g_gain1, g_shift1 = norm_back(d_hidden, resid1, gain1)
    d_attn = grad1.astype(BF16)
    g_wout = dot_tn(ctx, d_attn)
    g_bout = jnp.sum(d_attn.astype(F32), axis=0)
    d_ctx = dot_nt(d_attn, w_out).astype(BF16)
    d_q, d_k, d_v = attend_back(q, kv, d_ctx, lse, span, segq[None], segk[:, None], padk[:, None])
    g_wq = dot_tn(own, d_q)
    g_wk = dot_tn(wide, d_k)
    g_wv = dot_tn(wide, d_v)
    g_wqkv = jnp.concatenate([g_wq, g_wk, g_wv], axis=1)
    g_bq = jnp.sum(d_q.astype(F32), axis=0)
    g_bv = jnp.sum(d_v.astype(F32), axis=0)
    d_wide = dot_nt(d_k, w_qkv[:, width : 2 * width]) + dot_nt(d_v, w_qkv[:, 2 * width :])
    d_own = grad1 + dot_nt(d_q, w_qkv[:, :width])
    grads = (
        g_wqkv, g_bq, g_bv, g_wout, g_bout, g_gain1, g_shift1, g_wup, g_bup, g_wdown, g_bdown, g_gain2, g_shift2
    )
    return d_wide, d_own, grads


def per_device(
    hidden_in, cotangent, segments, pad_mask, w_qkv, b_query, b_value, w_out, b_out, norm1_gain, norm1_bias,
    w_up, b_up, w_down, b_down, norm2_gain, norm2_bias,
):
    shards = (
        w_qkv, b_query, b_value, w_out, b_out, norm1_gain, norm1_bias, w_up, b_up, w_down, b_down, norm2_gain, norm2_bias
    )
    place = Place()
    both, half, width = hidden_in.shape
    rows = 2 * half
    window = 8 * half
    full = tuple(lax.all_gather(shard, ("dp", "seq"), axis=0, tiled=True) for shard in shards)
    full = tuple(item if item.ndim == 2 else item.astype(F32) for item in full)
    spot = place.seq % LINE
    tags = jnp.stack([segments, pad_mask])
    other = lax.ppermute(tags, "dp", [(0, 1), (1, 0)])
    tags = jnp.where(place.core == spot // 2, tags, other)
    tags = jnp.where(spot % 2 == 0, tags[:, 0], tags[:, 1])
    offset = (2 * (place.seq // LINE) + place.core) * rows
    margin = REACH * half
    seg_all = jnp.pad(jnp.pad(tags[0], (margin, 0), constant_values=-1), (0, margin), constant_values=1 << 30)
    pad_all = jnp.pad(tags[1], (margin, margin))
    segk = lax.dynamic_slice_in_dim(seg_all, offset, window)
    padk = lax.dynamic_slice_in_dim(pad_all, offset, window)
    segq = segk[margin : margin + rows]
    padq = padk[margin : margin + rows]
    spans = []
    for tile in range(rows // TILE):
        first, last = segq[tile * TILE], segq[(tile + 1) * TILE - 1]
        low = jnp.sum((segk < first).astype(jnp.int32))
        high = jnp.sum((segk <= last).astype(jnp.int32))
        spans.append(jnp.stack([low // TILE, (high + TILE - 1) // TILE]))
    span = jnp.stack(spans)
    marks = (span, segq, segk, padk)
    own_in = place.take_in(hidden_in)
    own_ct = place.take_in(cotangent)
    state0 = own_in.astype(F32)
    state1, saved1 = forward_layer(place.widen(own_in), state0, full, marks)
    state2, saved2 = forward_layer(place.widen(state1.astype(BF16)), state1, full, marks)
    out = place.give_back(state2.astype(BF16))
    grad = own_ct.astype(F32) * padq[:, None].astype(F32)
    d_wide, d_own, grads2 = backward_layer(grad, full, saved2, marks)
    grad = d_own + place.narrow(d_wide)
    d_wide, d_own, grads1 = backward_layer(grad, full, saved1, marks)
    grad = d_own + place.narrow(d_wide)
    grad_in = place.give_back(grad.astype(BF16)).astype(F32)
    totals = jax.tree.map(lambda a, b: a + b, grads2, grads1)
    summed = tuple(lax.psum_scatter(item, ("dp", "seq"), scatter_dimension=0, tiled=True) for item in totals)
    return (out, grad_in) + summed


def solution(mesh):
    split = P(("dp", "seq"))
    mats = P(("dp", "seq"), None)
    tokens = P("dp", "seq", None)
    weights = (mats, split, split, mats, split, split, split, mats, split, mats, split, split, split)
    return jax.shard_map(
        per_device,
        mesh=mesh,
        in_specs=(tokens, tokens, P("dp", None), P("dp", None)) + weights,
        out_specs=(tokens, tokens) + weights,
        check_vma=False,
    )
```

time: 1880 us -> 1020 us (0.54)
  local copies, waits for them, and re-layouts: 362 us -> 31 us
  matrix products: 406 us -> 142 us
  waiting for transfers between devices: 597 us -> 452 us
  Pallas kernels: 0 us -> 125 us
  starting transfers between devices: 199 us -> 107 us
  other arithmetic: 117 us -> 32.5 us
  loops' own time: 81.6 us -> 0 us
    dot_general x216 -> x34, matrix products: 406 us -> 142 us  [the longest x12 52.9 us: dot_tn(): lax.dot_general(left, right, (((0,), (0,)), ((), ())), preferred_element_...]
    ppermute x48 -> x25, waiting for transfers between devices: 220 us -> 55 us  [the longest x16 55 us: move(): return lax.ppermute(block, ('dp', 'seq'), pairs)]
    dynamic_slice x196 -> x0, local copies, waits for them, and re-layouts: 146 us -> none  [the longest x48 40.8 us: group_slices(): lax.dynamic_slice_in_dim(projected, column, width, 1)]
    pallas_call x0 -> x4, Pallas kernels: none -> 125 us  [the longest x2 69.4 us: attend_back(): pl.pallas_call(attend_back_kernel, grid_spec=pltpu.PrefetchScalarGridSpec...]
    ppermute x48 -> x25, starting transfers between devices: 199 us -> 106 us  [the longest x16 94.9 us: move(): return lax.ppermute(block, ('dp', 'seq'), pairs)]
    another operation x8 -> x0, loops' own time: 81.6 us -> none  [the longest x4 64.6 us: backward_layer(): lax.map(attend_back, jnp.arange(HEADS // 2, dtype=jnp.int32))]
    unnamed x475 -> x244, local copies, waits for them, and re-layouts: 107 us -> 25.6 us
    dynamic_update_slice x72 -> x0, local copies, waits for them, and re-layouts: 41.3 us -> none  [the longest x48 37.3 us: backward_layer(): lax.map(attend_back, jnp.arange(HEADS // 2, dtype=jnp.int32))]
  transfers between devices with their start and end apart: 56 -> 33, of which waited for: 18 -> 13; matrix products, arithmetic and copies ran while one was open for 30% -> 13% of each run, Pallas kernels for 0% -> 6%
where the time goes in v1:
time: 1020 us; the launch traced here: 1010 us
  waiting for transfers between devices  452 us (44%)
  matrix products  142 us (14%)
  Pallas kernels  125 us (12%)
  starting transfers between devices  107 us (10%)
  blocking collectives  99.8 us (10%)
  other arithmetic  32.5 us (3%)
  local copies, waits for them, and re-layouts  31 us (3%)
  between operations  22.8 us (2%)
    reduce_scatter x3, waiting for transfers between devices, per_device(): lax.psum_scatter(item, ('dp', 'seq'), scatter_dimension=0, tiled=True)  284 us
    unnamed x2, blocking collectives  99.8 us
    ppermute x16, starting transfers between devices, move(): return lax.ppermute(block, ('dp', 'seq'), pairs)  94.9 us
    all_gather x4, waiting for transfers between devices, per_device(): lax.all_gather(shard, ('dp', 'seq'), axis=0, tiled=True)  88.6 us
    pallas_call x2, Pallas kernels, attend_back(): pl.pallas_call(attend_back_kernel, grid_spec=pltpu.PrefetchScalarGridSpec...  69.4 us
    pallas_call x2, Pallas kernels, attend(): pl.pallas_call(attend_kernel, grid_spec=pltpu.PrefetchScalarGridSpec(num_...  55.4 us
    ppermute x16, waiting for transfers between devices, move(): return lax.ppermute(block, ('dp', 'seq'), pairs)  55 us
    dot_general x12, matrix products, dot_tn(): lax.dot_general(left, right, (((0,), (0,)), ((), ())), preferred_element_...  52.9 us
  transfers between devices with their start and end apart: 33, of which 13 were waited for; matrix products, arithmetic and copies ran while one was open for 13% of the time, Pallas kernels for 6%

profile of v1, /device:TPU:0, one launch (start us, length us, event | category | flops | bytes accessed | tf_op | source)
XLA Modules:
  0.0 1011.6 jit_solution(5765904555589740080)
XLA Ops:
  16.9 4.5 collective-permute-start.14
  23.5 48.2 %all-reduce.23 = (bf16[768]{0:T(1024)(128)(2,1)S(1)}, bf16[768]{0:T(1024)(128)(2,1)S(1)}, bf16[768]{0:T(1024)(128)(2,1)S(1)}, bf16[768]{0:T(1024)(128)(2,1)S(1)}...) all-reduce(bf16[768]{0:T(1024)(128)(2,1)S(1)} %dynamic-update-slice, ...), channel_id=1, replica_groups=mesh['dp'=2,'seq'=16] {'dp','seq'}, use_global_device_ids=true, to_apply=%add.4 | all-reduce | flops 9216 | bytes 36864
  79.0 3.3 convert_reduce_fusion.13
  92.4 3.0 collective-permute-start.3
  98.8 6.4 collective-permute-done.3
  111.3 8.9 collective-permute-done.6
  121.0 3.1 multiply_convert_fusion.3.q_ref
  124.1 9.0 add_convert_fusion.1.k_ref.v_ref
  133.1 27.7 %attend.2 = (bf16[512,768]{1,0:T(8,128)(2,1)}, f32[6,8,512]{2,1,0:T(8,128)}) custom-call(s32[2,2]{1,0:T(2,128)} %pad_add_fusion.1.span, bf16[512,768]{1,0:T(8,128)(2,1)} %multiply_convert_fusion.3.q_ref, bf16[2048,1536]{1,0:T(8,128)(2,1)} %add_convert_fusion.1.k_ref.v_ref, bf16[2048,1536]{1,0:T(8,128)(2,1)} %add_convert_fusion.1.k_ref.v_ref, ...), custom_call_target="tpu_custom_call" | custom-call | tf_op jit(solution)/shard_map/attend/pallas_call | solution.py:108
  163.6 31.7 %all-gather.9.cloned.1.call-done = bf16[768,3072]{1,0:T(8,128)(2,1)} async-done(((bf16[24,3072]{1,0:T(8,128)(2,1)}), bf16[768,3072]{1,0:T(8,128)(2,1)}) %all-gather.9.cloned.1.call-update) | async-done | bytes 4718608 | tf_op jit(solution)/shard_map/all_gather | solution.py:396
  195.3 8.2 multiply_convert_fusion.1
  203.5 56.9 %all-gather.11.cloned.1.call-done = bf16[3072,768]{1,0:T(8,128)(2,1)} async-done(((bf16[96,768]{1,0:T(8,128)(2,1)}), bf16[3072,768]{1,0:T(8,128)(2,1)}) %all-gather.11.cloned.1.call-update) | async-done | bytes 4718608 | tf_op jit(solution)/shard_map/all_gather | solution.py:396
  260.4 6.1 fusion.71
  270.0 3.8 collective-permute-start.7
  280.2 3.1 collective-permute-done.7
  283.9 14.3 %collective-permute-done.10 = bf16[256,768]{1,0:T(8,128)(2,1)S(1)} collective-permute-done((bf16[256,768]{1,0:T(8,128)(2,1)S(1)}, bf16[256,768]{1,0:T(8,128)(2,1)S(1)}, u32[]{:S(2)}, u32[]{:S(2)}) %collective-permute-start.10) | collective-permute-done | bytes 393248 | tf_op jit(solution)/shard_map/ppermute | solution.py:282
  299.9 7.3 add_convert_fusion.k_ref.v_ref
  307.1 27.6 %attend.3 = (bf16[512,768]{1,0:T(8,128)(2,1)}, f32[6,8,512]{2,1,0:T(8,128)}) custom-call(s32[2,2]{1,0:T(2,128)} %pad_add_fusion.1.span, bf16[512,768]{1,0:T(8,128)(2,1)} %multiply_convert_fusion.2.q_ref, bf16[2048,1536]{1,0:T(8,128)(2,1)} %add_convert_fusion.k_ref.v_ref, bf16[2048,1536]{1,0:T(8,128)(2,1)} %add_convert_fusion.k_ref.v_ref, ...), custom_call_target="tpu_custom_call" | custom-call | tf_op jit(solution)/shard_map/attend/pallas_call | solution.py:108
  337.9 6.5 multiply_convert_fusion
  352.4 5.5 convert_reduce_fusion.1
  357.9 3.6 multiply_reduce_fusion.3
  364.6 34.8 %attend_back.2 = (bf16[512,768]{1,0:T(8,128)(2,1)}, bf16[2048,768]{1,0:T(8,128)(2,1)}, bf16[2048,768]{1,0:T(8,128)(2,1)}) custom-call(s32[2,2]{1,0:T(2,128)} %pad_add_fusion.1.span, bf16[512,768]{1,0:T(8,128)(2,1)} %multiply_convert_fusion.2.q_ref, bf16[2048,1536]{1,0:T(8,128)(2,1)} %add_convert_fusion.k_ref.v_ref, ...), custom_call_target="tpu_custom_call" | custom-call | tf_op jit(solution)/shard_map/attend_back/pallas_call | solution.py:213
  399.4 7.0 fusion.77
  413.4 29.7 %collective-permute-start.16 = (bf16[512,768]{1,0:T(8,128)(2,1)S(1)}, bf16[512,768]{1,0:T(8,128)(2,1)S(1)}, u32[]{:S(2)}, u32[]{:S(2)}) collective-permute-start(bf16[512,768]{1,0:T(8,128)(2,1)S(1)} %get-tuple-element.135), channel_id=1, source_target_pairs={{0,16},{16,4},{1,17},{17,5},{2,18},{18,6},{3,19},{19,7},{4,20},{20... | collective-permute-start | bytes 2359304 | tf_op jit(solution)/shard_map/ppermute | solution.py:282
  443.2 3.5 collective-permute-start.17
  451.1 5.1 collective-permute-done.17
  456.2 6.0 collective-permute-done.18
  465.6 7.9 convert_reduce_fusion
  473.5 3.7 multiply_reduce_fusion.2
  481.8 6.2 fusion.78
  489.7 34.6 %attend_back.3 = (bf16[512,768]{1,0:T(8,128)(2,1)}, bf16[2048,768]{1,0:T(8,128)(2,1)}, bf16[2048,768]{1,0:T(8,128)(2,1)}) custom-call(s32[2,2]{1,0:T(2,128)} %pad_add_fusion.1.span, bf16[512,768]{1,0:T(8,128)(2,1)} %multiply_convert_fusion.3.q_ref, bf16[2048,1536]{1,0:T(8,128)(2,1)} %add_convert_fusion.1.k_ref.v_ref, ...), custom_call_target="tpu_custom_call" | custom-call | tf_op jit(solution)/shard_map/attend_back/pallas_call | solution.py:213
  526.7 5.0 fusion.79
  531.7 4.9 fusion.80
  536.7 3.5 maximum_add_fusion
  540.2 8.0 copy.47
  548.9 5.5 fusion.55
  554.4 6.1 convolution_add_fusion.1
  560.6 5.2 fusion.52
  565.9 5.3 convolution_add_fusion
  575.3 4.8 fusion.29
  584.4 23.8 %collective-permute-start.20 = (bf16[512,768]{1,0:T(8,128)(2,1)S(1)}, bf16[512,768]{1,0:T(8,128)(2,1)S(1)}, u32[]{:S(2)}, u32[]{:S(2)}) collective-permute-start(bf16[512,768]{1,0:T(8,128)(2,1)S(1)} %get-tuple-element.131), channel_id=1, source_target_pairs={{0,16},{16,4},{1,17},{17,5},{2,18},{18,6},{3,19},{19,7},{4,20},{20... | collective-permute-start | bytes 2359304 | tf_op jit(solution)/shard_map/ppermute | solution.py:282
  608.4 15.4 %collective-permute-start.21 = (bf16[256,768]{1,0:T(8,128)(2,1)S(1)}, bf16[256,768]{1,0:T(8,128)(2,1)S(1)}, u32[]{:S(2)}, u32[]{:S(2)}) collective-permute-start(bf16[256,768]{1,0:T(8,128)(2,1)S(1)} %get-tuple-element.128), channel_id=1, source_target_pairs={{0,4},{16,20},{1,5},{17,21},{2,6},{18,22},{3,7},{19,23},{4,8},{20,... | collective-permute-start | bytes 1179656 | tf_op jit(solution)/shard_map/ppermute | solution.py:282
  626.8 5.5 collective-permute-done.21
  632.3 5.6 collective-permute-done.22
  640.7 51.6 %all-reduce.22 = (f32[768]{0:T(1024)S(1)}, f32[768]{0:T(1024)S(1)}, f32[768]{0:T(1024)S(1)}, f32[768]{0:T(1024)S(1)}, f32[768]{0:T(1024)S(1)}, /*index=5*/f32[30...) all-reduce(f32[768]{0:T(1024)S(1)} %add.366, ...), channel_id=3, replica_groups=mesh['dp'=2,'seq'=16] {'dp','seq'}, use_global_device_ids=true, to_apply=%region_23.24.clone | all-reduce | flops 9216 | bytes 73728
  698.9 21.8 %reduce-scatter.13.cloned.1.call-done = f32[24,2304]{1,0:T(8,128)} async-done(((f32[768,2304]{1,0:T(8,128)}), f32[24,2304]{1,0:T(8,128)}) %reduce-scatter.13.cloned.1.call-update) | async-done | bytes 221200
  720.8 141.3 %reduce-scatter.9.cloned.1.call-done = f32[24,3072]{1,0:T(8,128)} async-done(((f32[768,3072]{1,0:T(8,128)}), f32[24,3072]{1,0:T(8,128)}) %reduce-scatter.9.cloned.1.call-update) | async-done | bytes 294928 | tf_op jit(solution)/shard_map/reduce_scatter | solution.py:432
  862.1 142.2 %reduce-scatter.11.cloned.1.call-done = f32[96,768]{1,0:T(8,128)} async-done(((f32[3072,768]{1,0:T(8,128)}), f32[96,768]{1,0:T(8,128)}) %reduce-scatter.11.cloned.1.call-update) | async-done | bytes 294928 | tf_op jit(solution)/shard_map/reduce_scatter | solution.py:432
  (397 shorter events, 105.9 us)
Async XLA Ops:
  7.2 113.8 %all-gather.5.cloned.1.call-start = ((), (), s32[]{:S(2)}) async-start(), calls=%async_computation.4 | async-start | bytes 3649536 | tf_op jit(solution)/shard_map/all_gather | solution.py:396
  7.9 152.9 %all-gather.7.cloned.1.call-start = ((), (), s32[]{:S(2)}) async-start(), calls=%async_computation.5 | async-start | bytes 1216512 | tf_op jit(solution)/shard_map/all_gather | solution.py:396
  8.7 186.6 %all-gather.9.cloned.1.call-start = ((), (), s32[]{:S(2)}) async-start(), calls=%async_computation.6 | async-start | bytes 4866048 | tf_op jit(solution)/shard_map/all_gather | solution.py:396
  9.4 251.0 %all-gather.11.cloned.1.call-start = ((), (), s32[]{:S(2)}) async-start(), calls=%async_computation.7 | async-start | bytes 4866048 | tf_op jit(solution)/shard_map/all_gather | solution.py:396
  10.0 689.0 %reduce-scatter.7.cloned.1.call-start = ((), (), s32[]{:S(2)}) async-start(), calls=%async_computation.8 | async-start | bytes 2433024 | tf_op jit(solution)/shard_map/reduce_scatter | solution.py:432
  10.8 65.0 %collective-permute-start.2 = (s32[2,2,4096]{2,1,0:T(2,128)S(1)}, s32[2,2,4096]{2,1,0:T(2,128)S(1)}, u32[]{:S(2)}, u32[]{:S(2)}) collective-permute-start(s32[2,2,4096]{2,1,0:T(2,128)S(1)} %pad_add_fusion), channel_id=1, source_target_pairs={{0,16},{16,0},{1,17},{17,1},{2,18},{18,2},{3,19},{19,3},{4,20},{20... | collective-permute-start | bytes 196616 | tf_op jit(solution)/shard_map/ppermute | solution.py:400
  11.3 64.5 %copy-start.39 = (s32[2,4096]{1,0:T(2,128)S(1)}, s32[2,4096]{1,0:T(2,128)}, u32[]{:S(2)}) copy-start(s32[2,4096]{1,0:T(2,128)} %param.20) | copy-start | bytes 98308
  11.3 64.5 %copy-start.40 = (s32[2,4096]{1,0:T(2,128)S(1)}, s32[2,4096]{1,0:T(2,128)}, u32[]{:S(2)}) copy-start(s32[2,4096]{1,0:T(2,128)} %param.19) | copy-start | bytes 98308
  12.6 63.4 %collective-permute-start = (bf16[256,768]{1,0:T(8,128)(2,1)S(1)}, bf16[256,768]{1,0:T(8,128)(2,1)S(1)}, u32[]{:S(2)}, u32[]{:S(2)}) collective-permute-start(bf16[256,768]{1,0:T(8,128)(2,1)S(1)} %get-tuple-element.153), channel_id=1, source_target_pairs={{0,1},{16,3},{1,0},{17,2},{2,17},{18,19},{3,16},{19,18},{4,5},{20,... | collective-permute-start | bytes 1179656 | tf_op jit(solution)/shard_map/ppermute | solution.py:297
  15.2 60.9 %collective-permute-start.1 = (bf16[256,768]{1,0:T(8,128)(2,1)S(1)}, bf16[256,768]{1,0:T(8,128)(2,1)S(1)}, u32[]{:S(2)}, u32[]{:S(2)}) collective-permute-start(bf16[256,768]{1,0:T(8,128)(2,1)S(1)} %get-tuple-element.154), channel_id=1, source_target_pairs={{0,0},{16,2},{1,1},{17,3},{2,16},{18,18},{3,17},{19,19},{4,4},{20,... | collective-permute-start | bytes 1179656 | tf_op jit(solution)/shard_map/ppermute | solution.py:297
  16.8 257.0 %collective-permute-start.13 = (bf16[256,768]{1,0:T(8,128)(2,1)}, bf16[256,768]{1,0:T(8,128)(2,1)}, u32[]{:S(2)}, u32[]{:S(2)}) collective-permute-start(bf16[256,768]{1,0:T(8,128)(2,1)} %get-tuple-element.143), channel_id=1, source_target_pairs={{0,1},{16,3},{1,0},{17,2},{2,17},{18,19},{3,16},{19,18},{4,5},{20,... | collective-permute-start | bytes 1179656 | tf_op jit(solution)/shard_map/ppermute | solution.py:297
  16.9 257.0 %collective-permute-start.14 = (bf16[256,768]{1,0:T(8,128)(2,1)}, bf16[256,768]{1,0:T(8,128)(2,1)}, u32[]{:S(2)}, u32[]{:S(2)}) collective-permute-start(bf16[256,768]{1,0:T(8,128)(2,1)} %get-tuple-element.144), channel_id=1, source_target_pairs={{0,0},{16,2},{1,1},{17,3},{2,16},{18,18},{3,17},{19,19},{4,4},{20,... | collective-permute-start | bytes 1179656 | tf_op jit(solution)/shard_map/ppermute | solution.py:297
  76.1 84.7 %copy-start.20 = (bf16[256,768]{1,0:T(8,128)(2,1)}, bf16[256,768]{1,0:T(8,128)(2,1)S(1)}, u32[]{:S(2)}) copy-start(bf16[256,768]{1,0:T(8,128)(2,1)S(1)} %get-tuple-element.152) | copy-start | bytes 1179652
  76.6 31.2 %collective-permute-start.4 = (bf16[512,768]{1,0:T(8,128)(2,1)S(1)}, bf16[512,768]{1,0:T(8,128)(2,1)S(1)}, u32[]{:S(2)}, u32[]{:S(2)}) collective-permute-start(bf16[512,768]{1,0:T(8,128)(2,1)S(1)} %pad_maximum_fusion), channel_id=1, source_target_pairs={{0,16},{16,4},{1,17},{17,5},{2,18},{18,6},{3,19},{19,7},{4,20},{20... | collective-permute-start | bytes 2359304 | tf_op jit(solution)/shard_map/ppermute | solution.py:282
  92.4 12.8 %collective-permute-start.3 = (bf16[256,768]{1,0:T(8,128)(2,1)S(1)}, bf16[256,768]{1,0:T(8,128)(2,1)S(1)}, u32[]{:S(2)}, u32[]{:S(2)}) collective-permute-start(bf16[256,768]{1,0:T(8,128)(2,1)S(1)} %get-tuple-element.152), channel_id=1, source_target_pairs={{0,4},{16,20},{1,5},{17,21},{2,6},{18,22},{3,7},{19,23},{4,8},{20,... | collective-permute-start | bytes 1179656 | tf_op jit(solution)/shard_map/ppermute | solution.py:282
  95.5 14.9 %collective-permute-start.5 = (bf16[512,768]{1,0:T(8,128)(2,1)S(1)}, bf16[512,768]{1,0:T(8,128)(2,1)S(1)}, u32[]{:S(2)}, u32[]{:S(2)}) collective-permute-start(bf16[512,768]{1,0:T(8,128)(2,1)S(1)} %pad_maximum_fusion), channel_id=1, source_target_pairs={{16,0},{17,1},{18,2},{19,3},{4,16},{20,4},{5,17},{21,5},{6,18},{22... | collective-permute-start | bytes 2359304 | tf_op jit(solution)/shard_map/ppermute | solution.py:282
  105.2 15.0 %collective-permute-start.6 = (bf16[256,768]{1,0:T(8,128)(2,1)S(1)}, bf16[256,768]{1,0:T(8,128)(2,1)S(1)}, u32[]{:S(2)}, u32[]{:S(2)}) collective-permute-start(bf16[256,768]{1,0:T(8,128)(2,1)S(1)} %get-tuple-element.151), channel_id=1, source_target_pairs={{4,0},{20,16},{5,1},{21,17},{6,2},{22,18},{7,3},{23,19},{8,4},{24,... | collective-permute-start | bytes 1179656 | tf_op jit(solution)/shard_map/ppermute | solution.py:282
  133.1 27.8 %copy-start.79 = (f32[768]{0:T(1024)S(1)}, f32[768]{0:T(1024)}, u32[]{:S(2)}) copy-start(f32[768]{0:T(1024)} %convert_element_type.169) | copy-start | bytes 9220
  163.2 314.0 %copy-start.4 = (f32[512,768]{1,0:T(8,128)}, f32[512,768]{1,0:T(8,128)S(1)}, u32[]{:S(2)}) copy-start(f32[512,768]{1,0:T(8,128)S(1)} %get-tuple-element.127) | copy-start | bytes 4718596
  163.2 32.0 %copy-start.42 = (f32[768]{0:T(1024)S(1)}, f32[768]{0:T(1024)}, u32[]{:S(2)}) copy-start(f32[768]{0:T(1024)} %convert_element_type.171) | copy-start | bytes 9220
  163.2 32.0 %copy-start.63 = (f32[3072]{0:T(1024)S(1)}, f32[3072]{0:T(1024)}, u32[]{:S(2)}) copy-start(f32[3072]{0:T(1024)} %convert_element_type.173) | copy-start | bytes 36868
  163.3 97.1 %copy-start.44 = (f32[512]{0:T(512)}, f32[512]{0:T(512)S(1)}, u32[]{:S(2)}) copy-start(f32[512]{0:T(512)S(1)} %broadcast_multiply_fusion.11) | copy-start | bytes 6148
  163.6 39.9 %copy-start.50 = (f32[512]{0:T(512)}, f32[512]{0:T(512)S(1)}, u32[]{:S(2)}) copy-start(f32[512]{0:T(512)S(1)} %add_rsqrt_fusion.3) | copy-start | bytes 6148
  267.5 15.9 %collective-permute-start.8 = (bf16[512,768]{1,0:T(8,128)(2,1)S(1)}, bf16[512,768]{1,0:T(8,128)(2,1)S(1)}, u32[]{:S(2)}, u32[]{:S(2)}) collective-permute-start(bf16[512,768]{1,0:T(8,128)(2,1)S(1)} %fusion.25), channel_id=1, source_target_pairs={{0,16},{16,4},{1,17},{17,5},{2,18},{18,6},{3,19},{19,7},{4,20},{20... | collective-permute-start | bytes 2359304 | tf_op jit(solution)/shard_map/ppermute | solution.py:282
  270.0 13.3 %collective-permute-start.7 = (bf16[256,768]{1,0:T(8,128)(2,1)S(1)}, bf16[256,768]{1,0:T(8,128)(2,1)S(1)}, u32[]{:S(2)}, u32[]{:S(2)}) collective-permute-start(bf16[256,768]{1,0:T(8,128)(2,1)S(1)} %get-tuple-element.150), channel_id=1, source_target_pairs={{0,4},{16,20},{1,5},{17,21},{2,6},{18,22},{3,7},{19,23},{4,8},{20,... | collective-permute-start | bytes 1179656 | tf_op jit(solution)/shard_map/ppermute | solution.py:282
  275.9 7.9 collective-permute-start.9
  277.2 21.0 %collective-permute-start.10 = (bf16[256,768]{1,0:T(8,128)(2,1)S(1)}, bf16[256,768]{1,0:T(8,128)(2,1)S(1)}, u32[]{:S(2)}, u32[]{:S(2)}) collective-permute-start(bf16[256,768]{1,0:T(8,128)(2,1)S(1)} %get-tuple-element.149), channel_id=1, source_target_pairs={{4,0},{20,16},{5,1},{21,17},{6,2},{22,18},{7,3},{23,19},{8,4},{24,... | collective-permute-start | bytes 1179656 | tf_op jit(solution)/shard_map/ppermute | solution.py:282
  337.2 24.4 %copy-start.17 = (f32[512,768]{1,0:T(8,128)}, f32[512,768]{1,0:T(8,128)S(1)}, u32[]{:S(2)}) copy-start(f32[512,768]{1,0:T(8,128)S(1)} %get-tuple-element.166) | copy-start | bytes 4718596
  337.2 24.4 %copy-start.55 = (f32[512]{0:T(512)}, f32[512]{0:T(512)S(1)}, u32[]{:S(2)}) copy-start(f32[512]{0:T(512)S(1)} %broadcast_multiply_fusion.9) | copy-start | bytes 6148
  337.9 23.7 %copy-start.68 = (f32[512]{0:T(512)}, f32[512]{0:T(512)S(1)}, u32[]{:S(2)}) copy-start(f32[512]{0:T(512)S(1)} %add_rsqrt_fusion.1) | copy-start | bytes 6148
  411.9 36.1 %copy-start.11 = (bf16[512,768]{1,0:T(8,128)(2,1)S(1)}, bf16[512,768]{1,0:T(8,128)(2,1)}, u32[]{:S(2)}) copy-start(bf16[512,768]{1,0:T(8,128)(2,1)} %copy-done.10) | copy-start | bytes 2359300
  411.9 36.1 %copy-start.30 = (bf16[512,768]{1,0:T(8,128)(2,1)S(1)}, bf16[512,768]{1,0:T(8,128)(2,1)}, u32[]{:S(2)}) copy-start(bf16[512,768]{1,0:T(8,128)(2,1)} %get-tuple-element.28) | copy-start | bytes 2359300
  411.9 50.3 %collective-permute-start.15 = (bf16[512,768]{1,0:T(8,128)(2,1)S(1)}, bf16[512,768]{1,0:T(8,128)(2,1)S(1)}, u32[]{:S(2)}, u32[]{:S(2)}) collective-permute-start(bf16[512,768]{1,0:T(8,128)(2,1)S(1)} %get-tuple-element.134), channel_id=1, source_target_pairs={{16,0},{17,1},{18,2},{19,3},{4,16},{20,4},{5,17},{21,5},{6,18},{22... | collective-permute-start | bytes 2359304 | tf_op jit(solution)/shard_map/ppermute | solution.py:282
  413.4 48.9 %collective-permute-start.16 = (bf16[512,768]{1,0:T(8,128)(2,1)S(1)}, bf16[512,768]{1,0:T(8,128)(2,1)S(1)}, u32[]{:S(2)}, u32[]{:S(2)}) collective-permute-start(bf16[512,768]{1,0:T(8,128)(2,1)S(1)} %get-tuple-element.135), channel_id=1, source_target_pairs={{0,16},{16,4},{1,17},{17,5},{2,18},{18,6},{3,19},{19,7},{4,20},{20... | collective-permute-start | bytes 2359304 | tf_op jit(solution)/shard_map/ppermute | solution.py:282
  443.2 13.1 %collective-permute-start.17 = (bf16[256,768]{1,0:T(8,128)(2,1)S(1)}, bf16[256,768]{1,0:T(8,128)(2,1)S(1)}, u32[]{:S(2)}, u32[]{:S(2)}) collective-permute-start(bf16[256,768]{1,0:T(8,128)(2,1)S(1)} %get-tuple-element.132), channel_id=1, source_target_pairs={{0,4},{16,20},{1,5},{17,21},{2,6},{18,22},{3,7},{19,23},{4,8},{20,... | collective-permute-start | bytes 1179656 | tf_op jit(solution)/shard_map/ppermute | solution.py:282
  446.7 15.6 %collective-permute-start.18 = (bf16[256,768]{1,0:T(8,128)(2,1)S(1)}, bf16[256,768]{1,0:T(8,128)(2,1)S(1)}, u32[]{:S(2)}, u32[]{:S(2)}) collective-permute-start(bf16[256,768]{1,0:T(8,128)(2,1)S(1)} %get-tuple-element.133), channel_id=1, source_target_pairs={{4,0},{20,16},{5,1},{21,17},{6,2},{22,18},{7,3},{23,19},{8,4},{24,... | collective-permute-start | bytes 1179656 | tf_op jit(solution)/shard_map/ppermute | solution.py:282
  481.7 239.1 %reduce-scatter.13.cloned.1.call-start = ((), (), s32[]{:S(2)}) async-start(), calls=%async_computation.11 | async-start | bytes 7299072
  548.2 313.9 %reduce-scatter.9.cloned.1.call-start = ((), (), s32[]{:S(2)}) async-start(), calls=%async_computation.9 | async-start | bytes 9732096 | tf_op jit(solution)/shard_map/reduce_scatter | solution.py:432
  560.6 443.7 %reduce-scatter.11.cloned.1.call-start = ((), (), s32[]{:S(2)}) async-start(), calls=%async_computation.10 | async-start | bytes 9732096 | tf_op jit(solution)/shard_map/reduce_scatter | solution.py:432
  572.6 51.3 %collective-permute-start.11 = (bf16[256,768]{1,0:T(8,128)(2,1)S(1)}, bf16[256,768]{1,0:T(8,128)(2,1)S(1)}, u32[]{:S(2)}, u32[]{:S(2)}) collective-permute-start(bf16[256,768]{1,0:T(8,128)(2,1)S(1)} %get-tuple-element.147), channel_id=1, source_target_pairs={{0,0},{2,16},{1,1},{3,17},{16,2},{18,18},{17,3},{19,19},{4,4},{6,2... | collective-permute-start | bytes 1179656 | tf_op jit(solution)/shard_map/ppermute | solution.py:308
  573.3 52.3 %collective-permute-start.12 = (bf16[256,768]{1,0:T(8,128)(2,1)S(1)}, bf16[256,768]{1,0:T(8,128)(2,1)S(1)}, u32[]{:S(2)}, u32[]{:S(2)}) collective-permute-start(bf16[256,768]{1,0:T(8,128)(2,1)S(1)} %get-tuple-element.148), channel_id=1, source_target_pairs={{1,0},{3,16},{0,1},{2,17},{17,2},{19,18},{16,3},{18,19},{5,4},{7,2... | collective-permute-start | bytes 1179656 | tf_op jit(solution)/shard_map/ppermute | solution.py:308
  582.8 25.4 %copy-start.31 = (bf16[512,768]{1,0:T(8,128)(2,1)S(1)}, bf16[512,768]{1,0:T(8,128)(2,1)}, u32[]{:S(2)}) copy-start(bf16[512,768]{1,0:T(8,128)(2,1)} %get-tuple-element.28) | copy-start | bytes 2359300
  583.0 54.9 %collective-permute-start.19 = (bf16[512,768]{1,0:T(8,128)(2,1)S(1)}, bf16[512,768]{1,0:T(8,128)(2,1)S(1)}, u32[]{:S(2)}, u32[]{:S(2)}) collective-permute-start(bf16[512,768]{1,0:T(8,128)(2,1)S(1)} %get-tuple-element.130), channel_id=1, source_target_pairs={{16,0},{17,1},{18,2},{19,3},{4,16},{20,4},{5,17},{21,5},{6,18},{22... | collective-permute-start | bytes 2359304 | tf_op jit(solution)/shard_map/ppermute | solution.py:282
  584.4 53.5 %collective-permute-start.20 = (bf16[512,768]{1,0:T(8,128)(2,1)S(1)}, bf16[512,768]{1,0:T(8,128)(2,1)S(1)}, u32[]{:S(2)}, u32[]{:S(2)}) collective-permute-start(bf16[512,768]{1,0:T(8,128)(2,1)S(1)} %get-tuple-element.131), channel_id=1, source_target_pairs={{0,16},{16,4},{1,17},{17,5},{2,18},{18,6},{3,19},{19,7},{4,20},{20... | collective-permute-start | bytes 2359304 | tf_op jit(solution)/shard_map/ppermute | solution.py:282
  608.4 23.9 %collective-permute-start.21 = (bf16[256,768]{1,0:T(8,128)(2,1)S(1)}, bf16[256,768]{1,0:T(8,128)(2,1)S(1)}, u32[]{:S(2)}, u32[]{:S(2)}) collective-permute-start(bf16[256,768]{1,0:T(8,128)(2,1)S(1)} %get-tuple-element.128), channel_id=1, source_target_pairs={{0,4},{16,20},{1,5},{17,21},{2,6},{18,22},{3,7},{19,23},{4,8},{20,... | collective-permute-start | bytes 1179656 | tf_op jit(solution)/shard_map/ppermute | solution.py:282
  624.0 13.9 %collective-permute-start.22 = (bf16[256,768]{1,0:T(8,128)(2,1)S(1)}, bf16[256,768]{1,0:T(8,128)(2,1)S(1)}, u32[]{:S(2)}, u32[]{:S(2)}) collective-permute-start(bf16[256,768]{1,0:T(8,128)(2,1)S(1)} %get-tuple-element.129), channel_id=1, source_target_pairs={{4,0},{20,16},{5,1},{21,17},{6,2},{22,18},{7,3},{23,19},{8,4},{24,... | collective-permute-start | bytes 1179656 | tf_op jit(solution)/shard_map/ppermute | solution.py:282
  639.0 58.6 %collective-permute-start.23 = (bf16[256,768]{1,0:T(8,128)(2,1)S(1)}, bf16[256,768]{1,0:T(8,128)(2,1)S(1)}, u32[]{:S(2)}, u32[]{:S(2)}) collective-permute-start(bf16[256,768]{1,0:T(8,128)(2,1)S(1)} %get-tuple-element.139), channel_id=1, source_target_pairs={{0,0},{2,16},{1,1},{3,17},{16,2},{18,18},{17,3},{19,19},{4,4},{6,2... | collective-permute-start | bytes 1179656 | tf_op jit(solution)/shard_map/ppermute | solution.py:308
  639.7 57.9 %collective-permute-start.24 = (bf16[256,768]{1,0:T(8,128)(2,1)S(1)}, bf16[256,768]{1,0:T(8,128)(2,1)S(1)}, u32[]{:S(2)}, u32[]{:S(2)}) collective-permute-start(bf16[256,768]{1,0:T(8,128)(2,1)S(1)} %get-tuple-element.140), channel_id=1, source_target_pairs={{1,0},{3,16},{0,1},{2,17},{17,2},{19,18},{16,3},{18,19},{5,4},{7,2... | collective-permute-start | bytes 1179656 | tf_op jit(solution)/shard_map/ppermute | solution.py:308
  (89 other events, 553.7 us)
Sparse Core Ops, SparseCore 0:
  10.9 62.9 all-gather.4
  76.8 52.8 all-gather.6
  132.6 62.5 all-gather.8
  198.0 62.3 all-gather.10
  481.8 108.6 reduce-scatter.6
  597.6 123.1 reduce-scatter.12
  727.2 134.8 reduce-scatter.8
  869.6 134.6 reduce-scatter.10
